TPU v7x, 128 devices: a whole 4x4x4 slice. The times are simulated.
128 devices in a mesh: blk: 4 (over x), tok: 32 (over y, z, core).
Axes of the slice: x: 4, y: 4, z: 4, core: 2. Of those that a mesh axis runs over, the one named last changes fastest.
Arguments:
- tokens: bfloat16 [32, 1024, 1664], P('tok', 'blk'), may hold values from -6 to 6
- segment_ids: int32 [32, 1024], P('tok'), may hold values from 0 to 31, as said below
- merge_index: int32 [32, 256, 4], P('tok'), may hold values from 0 to 1023, as said below
- segment_owner: int32 [32, 32], P('tok'), may hold values from 0 to 31, each once within a row
- ln1_gain: float32 [1664], replicated, may hold values from 0.1 to 1.9
- ln1_bias: float32 [1664], replicated, may hold values from -4 to 4
- w_qkv: bfloat16 [3, 1664, 1664], P(None, 'tok', 'blk'), may hold values from -0.15625 to 0.15625
- qkv_bias: float32 [3, 1664], P(None, 'blk'), may hold values from -6 to 6
- w_out: bfloat16 [1664, 1664], P('blk', 'tok'), may hold values from -0.15625 to 0.15625
- out_bias: float32 [1664], replicated, may hold values from -6 to 6
- ln2_gain: float32 [1664], replicated, may hold values from 0.1 to 1.9
- ln2_bias: float32 [1664], replicated, may hold values from -4 to 4
- w_fc1: bfloat16 [1664, 8192], P(None, 'blk'), may hold values from -0.15625 to 0.15625
- fc1_bias: float32 [8192], P('blk'), may hold values from -6 to 6
- w_fc2: bfloat16 [8192, 1664], P('blk'), may hold values from -0.0625 to 0.0625
- fc2_bias: float32 [1664], replicated, may hold values from -6 to 6
- ln3_gain: float32 [1664], replicated, may hold values from 0.1 to 1.9
- ln3_bias: float32 [1664], replicated, may hold values from -4 to 4
- w_proj: bfloat16 [6656, 1664], P('tok', 'blk'), may hold values from -0.078125 to 0.078125
- proj_bias: float32 [1664], P('blk'), may hold values from -6 to 6
Outputs:
- returned: bfloat16 [32, 32, 16, 1664], P('tok', None, None, 'blk')
Inputs may be any that keep to these rules, and one draw needn't show every extreme that they name: `segment_ids`: within a block each segment holds 4 to 64 tokens, one exactly 64; the four tokens of one row of merge_index share a segment. `merge_index`: the rows of one block name each token of the block exactly once. `segment_owner`: each block's row is a permutation of the owners.
All inputs are finite; a program needn't handle non-finite values.
Results may differ from a plain program's by a relative error of at most 0.015.
Values may be sent and summed in bfloat16 or wider, within the bound.
A program may use at most 128 MiB of HBM per device.

v0:
```python
import math

import jax
import jax.numpy as jnp
from jax import lax
from jax.sharding import PartitionSpec as P

HD = 104


EPS = 1e-06


def layer_norm(input_tensors, scales, offset):
    input_tensors = input_tensors.astype(jnp.float32)
    center = input_tensors - jnp.mean(input_tensors, axis=-1, keepdims=True)
    spread = jnp.mean(center * center, axis=-1, keepdims=True)
    return center * lax.rsqrt(spread + EPS) * scales + offset


def body(
    tokens,
    segment_ids,
    merge_index,
    segment_owner,
    ln1_gain,
    ln1_bias,
    w_qkv,
    qkv_bias,
    w_out,
    out_bias,
    ln2_gain,
    ln2_bias,
    w_fc1,
    fc1_bias,
    w_fc2,
    fc2_bias,
    ln3_gain,
    ln3_bias,
    w_proj,
    proj_bias,
):
    tok_block = tokens[0]
    row_count = tok_block.shape[0]
    model_width = tok_block.shape[1]
    head_cols = w_qkv.shape[2]
    heads_here = head_cols // HD
    normed_one = layer_norm(tok_block, ln1_gain, ln1_bias).astype(jnp.bfloat16)
    normed_all = lax.all_gather(normed_one, "blk", axis=0, tiled=True)
    all_rows = normed_all.shape[0]
    columns = normed_all
    projected_qkv = jnp.einsum(
        "td,cde->cte",
        columns,
        lax.all_gather(w_qkv, "tok", axis=1, tiled=True),
        preferred_element_type=jnp.float32,
    )
    projected_qkv = (projected_qkv + qkv_bias[:, None, :]).astype(jnp.bfloat16)
    projected_qkv = projected_qkv.reshape(3, all_rows, heads_here, HD)
    key_rows = projected_qkv[1]
    values = projected_qkv[2]
    segment_row = segment_ids[0]
    q_block = min(512, all_rows)
    block_count = all_rows // q_block
    query_rows = projected_qkv[0].reshape(block_count, q_block, heads_here, HD)
    query_segs = segment_row.reshape(block_count, q_block)
    score_scale = 1.0 / math.sqrt(HD)

    def attend(input_tensors):
        query_part, query_seg = input_tensors
        scores = (
            jnp.einsum("qhe,khe->hqk", query_part, key_rows, preferred_element_type=jnp.float32)
            * score_scale
        )
        allowed = query_seg[:, None] == segment_row[None, :]
        weights = jnp.where(allowed[None], jnp.exp(scores), 0.0)
        attn_probs = (weights / jnp.sum(weights, axis=-1, keepdims=True)).astype(jnp.bfloat16)
        mixed = jnp.einsum("hqk,khe->qhe", attn_probs, values, preferred_element_type=jnp.float32)
        return mixed.astype(jnp.bfloat16)

    attended = lax.map(attend, (query_rows, query_segs)).reshape(all_rows, head_cols)
    out_full = lax.all_gather(w_out, "tok", axis=1, tiled=True)
    attn_rows = lax.psum_scatter(
        jnp.dot(attended, out_full, preferred_element_type=jnp.float32).astype(jnp.bfloat16),
        "blk",
        scatter_dimension=0,
        tiled=True,
    ).astype(jnp.float32)
    after_attn = tok_block.astype(jnp.float32) + attn_rows + out_bias
    normed_two = layer_norm(after_attn, ln2_gain, ln2_bias).astype(jnp.bfloat16)
    pre_act = (
        jnp.dot(
            lax.all_gather(normed_two, "blk", axis=0, tiled=True),
            w_fc1,
            preferred_element_type=jnp.float32,
        )
        + fc1_bias
    )
    hidden_act = jax.nn.gelu(pre_act, approximate=False).astype(jnp.bfloat16)
    partial_sum = jnp.dot(hidden_act, w_fc2, preferred_element_type=jnp.float32)
    own_start = lax.axis_index("blk") * row_count
    own_rows = lax.dynamic_slice_in_dim(partial_sum, own_start, row_count, 0) + after_attn
    partial_sum = lax.dynamic_update_slice_in_dim(partial_sum, own_rows, own_start, 0)
    summed = lax.psum(partial_sum.astype(jnp.bfloat16), "blk").astype(jnp.float32)
    layer_all = (summed + fc2_bias).astype(jnp.bfloat16)
    final_all = layer_norm(layer_all, ln3_gain, ln3_bias).astype(jnp.bfloat16)
    merge_rows = merge_index[0]
    merged_count = merge_rows.shape[0]
    merged = jnp.take(final_all, merge_rows.reshape(-1), axis=0).reshape(
        merged_count, 4 * model_width
    )
    columns = merged
    projected = jnp.dot(
        columns,
        lax.all_gather(w_proj, "tok", axis=0, tiled=True),
        preferred_element_type=jnp.float32,
    )
    projected = (projected + proj_bias).astype(jnp.bfloat16)
    tok_count = lax.axis_size("tok")
    slot_cap = 2 * merged_count // tok_count
    owners_here = segment_owner[0]
    seg_rows = jnp.take(segment_row, merge_rows[:, 0])
    seg_match = (
        seg_rows[:, None] == jnp.arange(owners_here.shape[0], dtype=jnp.int32)[None, :]
    ).astype(jnp.int32)
    owner_rows = jnp.sum(seg_match * owners_here[None, :], axis=1)
    segment_matches = (
        owner_rows[:, None] == jnp.arange(tok_count, dtype=jnp.int32)[None, :]
    ).astype(jnp.int32)
    before = jnp.cumsum(segment_matches, axis=0) - segment_matches
    order_in = jnp.sum(before * segment_matches, axis=1)
    target = owner_rows * slot_cap + order_in
    placed = (jnp.arange(tok_count * slot_cap, dtype=jnp.int32)[:, None] == target[None, :]).astype(
        jnp.bfloat16
    )
    outgoing = jnp.dot(placed, projected, preferred_element_type=jnp.float32).astype(jnp.bfloat16)
    outgoing = outgoing.reshape(tok_count, slot_cap, projected.shape[1])
    arrived = lax.all_to_all(outgoing, "tok", split_axis=0, concat_axis=0, tiled=True)
    return arrived[None]


def solution(mesh):
    placed = (
        P("tok", "blk", None),
        P("tok", None),
        P("tok", None, None),
        P("tok", None),
        P(),
        P(),
        P(None, "tok", "blk"),
        P(None, "blk"),
        P("blk", "tok"),
        P(),
        P(),
        P(),
        P(None, "blk"),
        P("blk"),
        P("blk", None),
        P(),
        P(),
        P(),
        P("tok", "blk"),
        P("blk"),
    )
    return jax.shard_map(
        body, mesh=mesh, in_specs=placed, out_specs=P("tok", None, None, "blk"), check_vma=False
    )
```

profile of v0, /device:TPU:1, one launch (start us, length us, event | category | flops | bytes accessed | tf_op | source)
XLA Modules:
  0.0 480.8 jit_solution(5821261523930769322)
XLA Ops:
  6.5 0.7 all-gather.15.cloned.1.call-update
  7.3 1.3 convert_reduce_fusion.1
  8.7 1.5 fusion.43
  10.2 2.5 fusion.46
  12.8 1.7 copy.32
  14.6 0.5 broadcast.197
  15.1 1.3 reduce.6
  16.4 40.5 %all-gather.15.cloned.1.call-done = bf16[32,52,416]{2,1,0:T(8,128)(2,1)} async-done(((bf16[1,52,416]{2,1,0:T(8,128)(2,1)}), bf16[32,52,416]{2,1,0:T(8,128)(2,1)}) %all-gather.15.cloned.1.call-update) | async-done | bytes 1384464 | tf_op jit(solution)/shard_map/all_gather | solution.py:82
  56.9 2.7 reshape.179
  59.7 39.4 %all-gather.7.cloned.1.call-done = bf16[1024,1664]{1,0:T(8,128)(2,1)} async-done(((bf16[256,1664]{1,0:T(8,128)(2,1)}), bf16[1024,1664]{1,0:T(8,128)(2,1)}) %all-gather.7.cloned.1.call-update) | async-done | bytes 3407888 | tf_op jit(solution)/shard_map/all_gather | solution.py:49
  99.1 53.1 %all-gather.9.cloned.1.call-done = bf16[3,1664,416]{2,0,1:T(4,128)(2,1)} async-done(((bf16[3,52,416]{2,0,1:T(4,128)(2,1)}), bf16[3,1664,416]{2,0,1:T(4,128)(2,1)}) %all-gather.9.cloned.1.call-update) | async-done | bytes 4153360 | tf_op jit(solution)/shard_map/all_gather | solution.py:55
  152.2 9.2 %fusion.34 = bf16[3,1024,416]{1,2,0:T(8,128)(2,1)S(1)} fusion(f32[3,416]{1,0:T(4,128)S(1)} %copy-done.15, bf16[3,1664,416]{2,0,1:T(4,128)(2,1)} %all-gather.9.cloned.1.call-done, bf16[1024,1664]{1,0:T(8,128)(2,1)} %all-gather.7.cloned.1.call-done), kind=kOutput, calls=%fused_computation.53 | convolution fusion | flops 4255580160 | bytes 10122112 | tf_op jit(solution)/shard_map/td,cde->cte/dot_general | solution.py:52
  161.4 1.4 fusion.96
  162.8 0.6 reshape_squeeze.10
  163.4 1.0 copy.34
  164.4 15.8 %while.10 = (s32[]{:T(128)}, bf16[2,512,4,104]{1,3,2,0:T(8,128)(2,1)}, s32[2,512]{1,0:T(2,128)S(1)}, s32[1,1024]{1,0:T(1,128)S(1)}, bf16[2,512,4,104]{1,3,2,0:T(...) while((s32[]{:T(128)}, bf16[2,512,4,104]{1,3,2,0:T(8,128)(2,1)}, ...), condition=%wide.region_8.9_spmd, body=%wide.region_6.8_spmd.sunk | while | flops 887830528 | bytes 31156912 | solution.py:81
  164.8 4.0 fusion.112
  168.8 2.5 fusion.113
  171.3 0.9 copy-done.6
  172.6 4.0 fusion.112
  176.6 2.5 fusion.113
  179.2 0.9 copy-done.6
  180.2 2.0 copy.35
  182.4 3.9 convolution_convert_fusion
  186.4 38.9 %reduce-scatter.2.cloned.1.call-done = bf16[256,1664]{1,0:T(8,128)(2,1)} async-done(((bf16[1024,1664]{1,0:T(8,128)(2,1)}), bf16[256,1664]{1,0:T(8,128)(2,1)}) %reduce-scatter.2.cloned.1.call-update) | async-done | bytes 851984 | tf_op jit(solution)/shard_map/reduce_scatter | solution.py:83
  225.3 1.5 fusion.57
  226.9 1.7 multiply_reduce_fusion
  228.5 2.6 add_convert_fusion.2
  231.3 41.5 %all-gather.11.cloned.1.call-done = bf16[1024,1664]{1,0:T(8,128)(2,1)} async-done(((bf16[256,1664]{1,0:T(8,128)(2,1)}), bf16[1024,1664]{1,0:T(8,128)(2,1)}) %all-gather.11.cloned.1.call-update) | async-done | bytes 3407888 | tf_op jit(solution)/shard_map/all_gather | solution.py:93
  272.7 11.1 %fusion.97 = f32[1024,2048]{1,0:T(8,128)S(1)} fusion(bf16[1024,1664]{1,0:T(8,128)(2,1)} %all-gather.11.cloned.1.call-done, bf16[1664,2048]{1,0:T(8,128)(2,1)} %param.34), kind=kOutput, calls=%fused_computation.133 | convolution fusion | flops 6979321856 | bytes 18612224 | tf_op jit(solution)/shard_map/dot_general | solution.py:92
  283.9 28.8 %fusion.29 = f32[1024,1664]{1,0:T(8,128)S(1)} fusion(bf16[2048,1664]{1,0:T(8,128)(2,1)} %param.36, f32[1024,2048]{1,0:T(8,128)S(1)} %fusion.97, f32[2048]{0:T(1024)S(1)} %copy-done.16), kind=kOutput, calls=%fused_computation.48 | convolution fusion | flops 7117733888 | bytes 22028288 | tf_op jit(solution)/shard_map/dot_general | solution.py:100
  313.2 2.2 convert_element_type.78
  315.5 0.7 all-gather.13.cloned.1.call-update
  316.5 1.4 gather_fusion
  318.0 0.6 reduce-window.6
  319.0 0.9 broadcast_in_dim.40
  320.0 2.0 copy.39
  322.1 73.7 %all-reduce.2.cloned.1.call-done = bf16[1024,1664]{1,0:T(8,128)(2,1)} async-done(((bf16[1024,1664]{1,0:T(8,128)(2,1)}), bf16[1024,1664]{1,0:T(8,128)(2,1)}) %all-reduce.2.cloned.1.call-update) | async-done | bytes 3407888 | tf_op jit(solution)/shard_map/psum | solution.py:104
  395.8 2.8 convert_reduce_fusion
  398.7 3.2 fusion.23
  401.9 1.8 fusion.26
  403.7 5.9 %gather_fusion.1 = bf16[1024,1664]{1,0:T(8,128)(2,1)} fusion(bf16[1024,1664]{1,0:T(8,128)(2,1)S(1)} %fusion.26, s32[1024]{0:T(1024)S(1)} %broadcast_clamp_fusion), kind=kCustom, calls=%fused_computation.1 | custom fusion | bytes 6819840 | tf_op jit(solution)/shard_map/jit(_take)/gather | solution.py:109
  409.6 5.4 %gather.15 = bf16[256,6656]{1,0:T(8,128)(2,1)S(1)} reshape(bf16[1024,1664]{1,0:T(8,128)(2,1)} %gather_fusion.1) | data formatting | bytes 6815744 | tf_op jit(solution)/shard_map/jit(_take)/gather | solution.py:109
  415.0 33.5 %all-gather.13.cloned.1.call-done = bf16[6656,416]{1,0:T(8,128)(2,1)} async-done(((bf16[208,416]{1,0:T(8,128)(2,1)}), bf16[6656,416]{1,0:T(8,128)(2,1)}) %all-gather.13.cloned.1.call-update) | async-done | bytes 5537808 | tf_op jit(solution)/shard_map/all_gather | solution.py:115
  448.5 7.0 %convolution_convert_fusion.1 = bf16[512,416]{0,1:T(8,128)(2,1)} fusion(bf16[6656,416]{1,0:T(8,128)(2,1)} %all-gather.13.cloned.1.call-done, pred[256,6656]{1,0:T(8,128)(4,1)} %bitcast.118, bf16[256,6656]{1,0:T(8,128)(2,1)S(1)} %gather.15, s32[256]{0:T(256)S(1)} %multiply_add_fusion, f32[416]{0:T(512)S(1)} %copy-done.17), kind=kOutput, calls=%fused_computation.69 | convolution fusion | flops 1528987648 | bytes 11078272 | tf_op jit(solution)/shard_map/dot_general | solution.py:136
  455.5 1.2 copy.37
  456.7 16.2 %all_to_all.5 = bf16[32,16,416]{2,1,0:T(8,128)(2,1)S(1)} all-to-all(bf16[32,16,416]{2,1,0:T(8,128)(2,1)S(1)} %bitcast.116), channel_id=1, replica_groups=mesh['blk'=4,'tok'=32] {'tok'}, dimensions={0} | all-to-all | bytes 851968 | tf_op jit(solution)/shard_map/all_to_all | solution.py:138
  472.9 0.8 copy.56
  (82 shorter events, 2.7 us)
Async XLA Ops:
  6.5 145.7 %copy-start.15 = (f32[3,416]{1,0:T(4,128)S(1)}, f32[3,416]{1,0:T(4,128)}, u32[]{:S(2)}) copy-start(f32[3,416]{1,0:T(4,128)} %param.29) | copy-start | bytes 14980
  6.5 50.4 %all-gather.15.cloned.1.call-start = ((), (), s32[]{:S(2)}) async-start(), calls=%async_computation.8 | async-start | bytes 1892352 | tf_op jit(solution)/shard_map/all_gather | solution.py:82
  7.3 91.8 %all-gather.7.cloned.1.call-start = ((), (), s32[]{:S(2)}) async-start(), calls=%async_computation.2 | async-start | bytes 4259840 | tf_op jit(solution)/shard_map/all_gather | solution.py:49
  12.8 139.4 %all-gather.9.cloned.1.call-start = ((), (), s32[]{:S(2)}) async-start(), calls=%async_computation.3 | async-start | bytes 7028736 | tf_op jit(solution)/shard_map/all_gather | solution.py:55
  14.5 210.8 %reduce-scatter.2.cloned.1.call-start = ((), (), s32[]{:S(2)}) async-start(), calls=%async_computation.4 | async-start | bytes 4259840 | tf_op jit(solution)/shard_map/reduce_scatter | solution.py:83
  161.4 3.0 copy-start
  164.4 4.3 copy-start.4
  164.4 4.3 copy-start.5
  171.3 0.9 copy-start.6
  172.2 4.3 copy-start.4
  172.2 4.3 copy-start.5
  179.1 0.9 copy-start.6
  182.4 42.9 %copy-start.1 = (bf16[1,256,1664]{2,1,0:T(8,128)(2,1)S(1)}, bf16[1,256,1664]{2,1,0:T(8,128)(2,1)}, u32[]{:S(2)}) copy-start(bf16[1,256,1664]{2,1,0:T(8,128)(2,1)} %param.22) | copy-start | bytes 2555908
  182.4 42.9 %copy-start.7 = (f32[1664]{0:T(1024)S(1)}, f32[1664]{0:T(1024)}, u32[]{:S(2)}) copy-start(f32[1664]{0:T(1024)} %param.31) | copy-start | bytes 19972
  186.4 42.2 %copy-start.10 = (f32[1664]{0:T(1024)S(1)}, f32[1664]{0:T(1024)}, u32[]{:S(2)}) copy-start(f32[1664]{0:T(1024)} %param.33) | copy-start | bytes 19972
  186.4 42.2 %copy-start.11 = (f32[1664]{0:T(1024)S(1)}, f32[1664]{0:T(1024)}, u32[]{:S(2)}) copy-start(f32[1664]{0:T(1024)} %param.32) | copy-start | bytes 19972
  186.4 86.3 %all-gather.11.cloned.1.call-start = ((), (), s32[]{:S(2)}) async-start(), calls=%async_computation.5 | async-start | bytes 4259840 | tf_op jit(solution)/shard_map/all_gather | solution.py:93
  231.2 164.6 %all-reduce.2.cloned.1.call-start = ((), (), s32[]{:S(2)}) async-start(), calls=%async_computation.6 | async-start | bytes 6815744 | tf_op jit(solution)/shard_map/psum | solution.py:104
  231.2 52.6 %copy-start.16 = (f32[2048]{0:T(1024)S(1)}, f32[2048]{0:T(1024)}, u32[]{:S(2)}) copy-start(f32[2048]{0:T(1024)} %param.35) | copy-start | bytes 24580
  283.9 28.9 %copy-start.3 = (bf16[256,1664]{1,0:T(8,128)(2,1)S(1)}, bf16[256,1664]{1,0:T(8,128)(2,1)}, u32[]{:S(2)}) copy-start(bf16[256,1664]{1,0:T(8,128)(2,1)} %reduce-scatter.2.cloned.1.call-done) | copy-start | bytes 2555908
  313.2 3.0 copy-start.9
  313.2 4.7 copy-start.14
  315.4 80.4 %copy-start.8 = (f32[1664]{0:T(1024)S(1)}, f32[1664]{0:T(1024)}, u32[]{:S(2)}) copy-start(f32[1664]{0:T(1024)} %param.37) | copy-start | bytes 19972
  315.4 133.1 %all-gather.13.cloned.1.call-start = ((), (), s32[]{:S(2)}) async-start(), calls=%async_computation.7 | async-start | bytes 7028736 | tf_op jit(solution)/shard_map/all_gather | solution.py:115
  316.2 85.7 %copy-start.12 = (f32[1664]{0:T(1024)S(1)}, f32[1664]{0:T(1024)}, u32[]{:S(2)}) copy-start(f32[1664]{0:T(1024)} %param.39) | copy-start | bytes 19972
  316.2 85.6 %copy-start.13 = (f32[1664]{0:T(1024)S(1)}, f32[1664]{0:T(1024)}, u32[]{:S(2)}) copy-start(f32[1664]{0:T(1024)} %param.38) | copy-start | bytes 19972
  395.8 6.1 %copy-start.2 = (bf16[1024,1664]{1,0:T(8,128)(2,1)S(1)}, bf16[1024,1664]{1,0:T(8,128)(2,1)}, u32[]{:S(2)}) copy-start(bf16[1024,1664]{1,0:T(8,128)(2,1)} %all-reduce.2.cloned.1.call-done) | copy-start | bytes 10223620
  409.6 39.0 %copy-start.17 = (f32[416]{0:T(512)S(1)}, f32[416]{0:T(512)}, u32[]{:S(2)}) copy-start(f32[416]{0:T(512)} %param.41) | copy-start | bytes 4996
Sparse Core Ops, SparseCore 0:
  9.6 47.2 all-gather.14
  58.6 40.4 all-gather.6
  101.3 50.8 all-gather.8
  186.5 38.7 reduce-scatter.1
  231.3 41.3 all-gather.10
  315.5 80.1 all-reduce.1
  398.0 50.4 all-gather.12
where the time goes:
time: 490 us; the launch traced here: 481 us
  waiting for transfers between devices  322 us (66%)
  matrix products  73 us (15%)
  local copies, waits for them, and re-layouts  30.3 us (6%)
  other arithmetic  24.6 us (5%)
  blocking collectives  16.2 us (3%)
  between operations  14 us (3%)
    psum x1, waiting for transfers between devices, body(): lax.psum(partial_sum.astype(jnp.bfloat16), 'blk').astype(jnp.float32)  73.7 us
    all_gather x1, waiting for transfers between devices, body(): lax.all_gather(w_qkv, 'tok', axis=1, tiled=True)  53.1 us
    all_gather x1, waiting for transfers between devices, body(): lax.all_gather(normed_two, 'blk', axis=0, tiled=True)  41.5 us
    all_gather x1, waiting for transfers between devices, body(): out_full = lax.all_gather(w_out, 'tok', axis=1, tiled=True)  40.5 us
    all_gather x1, waiting for transfers between devices, body(): normed_all = lax.all_gather(normed_one, 'blk', axis=0, tiled=True)  39.4 us
    reduce_scatter x1, waiting for transfers between devices, body(): lax.psum_scatter(jnp.dot(attended, out_full, preferred_element_type=jnp.f...  38.9 us
    all_gather x1, waiting for transfers between devices, body(): lax.all_gather(w_proj, 'tok', axis=0, tiled=True)  33.5 us
    dot_general x1, matrix products, body(): partial_sum = jnp.dot(hidden_act, w_fc2, preferred_element_type=jnp.float32)  28.8 us
  transfers between devices with their start and end apart: 7, of which 7 were waited for; matrix products, arithmetic and copies ran while one was open for 8% of the time, Pallas kernels for 0%

commit v1 on v0

v1 whole, which is shorter than its diff:
```python
import math

import jax
import jax.numpy as jnp
from jax import lax
from jax.experimental import pallas as pl
from jax.experimental.pallas import tpu as pltpu
from jax.sharding import PartitionSpec as P

HD = 104
HPAD = 128
EPS = 1e-06
BF = jnp.bfloat16
F32 = jnp.float32
MESH_ID = pl.DeviceIdType.MESH
VLIM = 65000 * 1024
VM = pl.BlockSpec(memory_space=pltpu.VMEM)
ANY = pl.BlockSpec(memory_space=pl.ANY)


def position():
    x = lax.axis_index("blk")
    t = lax.axis_index("tok")
    return x, t // 8, (t // 2) % 4, t % 2


def tok_of(y, z, c):
    return ((y % 4) * 4 + z % 4) * 2 + c


def rcopy(src, dst, ssem, rsem, dev):
    return pltpu.make_async_remote_copy(
        src_ref=src, dst_ref=dst, send_sem=ssem, recv_sem=rsem, device_id=dev, device_id_type=MESH_ID
    )


def x_dev(x, off):
    return {"blk": (x + off) % 4}


def meet(peers):
    bar = pltpu.get_barrier_semaphore()
    for dev in peers:
        pl.semaphore_signal(bar, inc=1, device_id=dev, device_id_type=MESH_ID)
    pl.semaphore_wait(bar, len(peers))


def x_peers():
    x, y, z, c = position()
    return [x_dev(x, 1), x_dev(x, 3)]


def tok_peers():
    x, y, z, c = position()
    return [
        {"tok": tok_of(y, z + 1, c)},
        {"tok": tok_of(y, z + 3, c)},
        {"tok": tok_of(y + 1, z, c)},
        {"tok": tok_of(y + 3, z, c)},
        {"tok": tok_of(y, z, 1 - c)},
    ]


class RingGather:
    def __init__(self, own, half, ss, rs):
        x = lax.axis_index("blk")
        right, left = x_dev(x, 1), x_dev(x, 3)

        def send(view, src, i, k, dev):
            return rcopy(view, half(src, i), ss(k), rs(k), dev)

        me, lo, hi = x, (x + 3) % 4, (x + 1) % 4
        self.c = [
            send(own(0), me, 0, 0, right),
            send(own(1), me, 1, 1, right),
            send(own(1), me, 1, 2, left),
            send(own(0), me, 0, 3, left),
            send(half(lo, 0), lo, 0, 4, right),
            send(half(hi, 1), hi, 1, 5, left),
        ]

    def start(self):
        for k in (0, 2, 1, 3):
            self.c[k].start()

    def relay(self):
        self.c[0].wait_recv()
        self.c[4].start()
        self.c[2].wait_recv()
        self.c[5].start()

    def wait_near(self):
        self.c[1].wait_recv()
        self.c[3].wait_recv()

    def wait_far(self):
        self.c[4].wait_recv()
        self.c[5].wait_recv()

    def finish(self):
        for c in self.c:
            c.wait_send()


class TokGather:
    OFF = (0, 3, 1, 2)

    def __init__(self, own, slots, half, zs, zr, ys, yr, cs, cr):
        x, y, z, c = position()
        self.slots, self.half = slots, half
        self.pos = (y, z, c)
        me = tok_of(y, z, c)

        def dev(yy, zz, cc):
            return {"tok": tok_of(yy, zz, cc)}

        def slot(yy, zz):
            return slots.at[tok_of(yy, zz, c)]

        zp, zm = dev(y, z + 1, c), dev(y, z + 3, c)
        yp, ym = dev(y + 1, z, c), dev(y + 3, z, c)
        sib = dev(y, z, 1 - c)
        self.zc = [
            rcopy(own, slots.at[me], zs.at[0], zr.at[0], zp),
            rcopy(own, slots.at[me], zs.at[1], zr.at[1], zm),
            rcopy(half(slot(y, z + 3), 0), half(slot(y, z + 3), 0), zs.at[2], zr.at[2], zp),
            rcopy(half(slot(y, z + 1), 1), half(slot(y, z + 1), 1), zs.at[3], zr.at[3], zm),
        ]
        self.yc = []
        for i, o in enumerate(self.OFF):
            src = own if i == 0 else slot(y, z + o)
            here = slot(y, z + o)
            up, dn = slot(y + 3, z + o), slot(y + 1, z + o)
            self.yc.append(
                [
                    rcopy(src, here, ys.at[i, 0], yr.at[i, 0], yp),
                    rcopy(src, here, ys.at[i, 1], yr.at[i, 1], ym),
                    rcopy(half(up, 0), half(up, 0), ys.at[i, 2], yr.at[i, 2], yp),
                    rcopy(half(dn, 1), half(dn, 1), ys.at[i, 3], yr.at[i, 3], ym),
                ]
            )
        self.cc = []
        for dy in range(4):
            row = []
            for i, o in enumerate(self.OFF):
                s = slot(y + self.OFF[dy], z + o)
                src = own if (i == 0 and dy == 0) else s
                row.append(rcopy(src, s, cs.at[dy, i], cr.at[dy, i], sib))
            self.cc.append(row)

    def start(self):
        self.zc[0].start()
        self.zc[1].start()
        self._fan(0)

    def _fan(self, i):
        self.yc[i][0].start()
        self.yc[i][1].start()
        self.cc[0][i].start()

    def z_near(self):
        self.zc[0].wait_recv()
        self.zc[2].start()
        self._fan(1)
        self.zc[1].wait_recv()
        self.zc[3].start()
        self._fan(2)

    def z_far(self):
        self.zc[2].wait_recv()
        self.zc[3].wait_recv()
        self._fan(3)

    def y_near(self, i):
        self.yc[i][0].wait_recv()
        self.yc[i][2].start()
        self.cc[1][i].start()
        self.yc[i][1].wait_recv()
        self.yc[i][3].start()
        self.cc[2][i].start()

    def y_far(self, i):
        self.yc[i][2].wait_recv()
        self.yc[i][3].wait_recv()
        self.cc[3][i].start()

    def wait_all(self):
        for row in self.cc:
            for d in row:
                d.wait_recv()

    def finish(self):
        for d in self.zc:
            d.wait_send()
        for row in self.yc + self.cc:
            for d in row:
                d.wait_send()


TOK_SEMS = [pltpu.SemaphoreType.DMA((4,))] * 2 + [pltpu.SemaphoreType.DMA((4, 4))] * 4


def norm_rows(src, dst, gain, bias, rows, step=32):
    @pl.loop(0, rows // step)
    def _(i):
        at = pl.ds(pl.multiple_of(i * step, step), step)
        v = src[at, :].astype(F32)
        mean = jnp.mean(v, axis=-1, keepdims=True)
        center = v - mean
        spread = jnp.mean(center * center, axis=-1, keepdims=True)
        dst[at, :] = (center * lax.rsqrt(spread + EPS) * gain[...] + bias[...]).astype(dst.dtype)


def k_qkv(tok, wl, wo, gain, bias, qb, toks, qkv, wo4, slots, wf, hb, lsem, xs, xr, ws, wr, *gs):
    x, y, z, c = position()
    t = lax.axis_index("tok")
    meet(x_peers() + [x_dev(x, 2)] + tok_peers())
    ring = RingGather(
        lambda i: tok.at[pl.ds(128 * i, 128)],
        lambda s, i: toks.at[s, pl.ds(128 * i, 128)],
        lambda k: xs.at[k],
        lambda k: xr.at[k],
    )
    wide = wl.shape[1] // 2
    gath = TokGather(wl, slots, lambda r, i: r.at[:, pl.ds(wide * i, wide)], *gs)
    gath.start()
    ring.start()
    wo_send = [rcopy(wo, wo4.at[x], ws.at[k], wr.at[k], x_dev(x, k + 1)) for k in range(3)]
    for d in wo_send:
        d.start()
    local = [
        pltpu.make_async_copy(tok, toks.at[x], lsem.at[0]),
        pltpu.make_async_copy(wl, slots.at[t], lsem.at[1]),
        pltpu.make_async_copy(wo, wo4.at[x], lsem.at[2]),
    ]
    for d in local:
        d.start()
    norm_rows(tok, hb.at[x], gain, bias, 256)
    gath.z_near()
    gath.z_far()
    gath.y_near(0)
    ring.relay()
    for i in range(1, 4):
        gath.y_near(i)
    ring.wait_near()
    for o in (1, 3):
        s = (x + o) % 4
        norm_rows(toks.at[s], hb.at[s], gain, bias, 256)
    for i in range(4):
        gath.y_far(i)
    for d in local:
        d.wait()
    gath.wait_all()

    @pl.loop(0, 8)
    def _(g):
        parts = [slots[4 * g + j] for j in range(4)]
        wf[pl.ds(pl.multiple_of(g * 208, 16), 208), :] = jnp.concatenate(parts, axis=0)

    def project(s):
        @pl.loop(0, wf.shape[1] // 256)
        def _(j):
            cols = pl.ds(pl.multiple_of(j * 256, 256), 256)
            v = jnp.dot(hb[s], wf[:, cols], preferred_element_type=F32) + qb[:, cols]
            v = v.astype(BF)
            rows = pl.ds(pl.multiple_of(s * 256, 256), 256)
            qkv[2 * j, rows, :] = v[:, :128]
            qkv[2 * j + 1, rows, :] = v[:, 128:]

    @pl.loop(0, 3)
    def _(i):
        project((x + i + i // 2) % 4)

    ring.wait_far()
    far = (x + 2) % 4
    norm_rows(toks.at[far], hb.at[far], gain, bias, 256)
    project(far)
    for d in wo_send:
        d.wait()
    ring.finish()
    gath.finish()


def k_att(qkv, segc, segr, wo4, att, wof, oh, slots, lsem, xs, xr, *gs):
    x, y, z, c = position()
    t = lax.axis_index("tok")
    meet(x_peers() + tok_peers())
    gath = TokGather(wo4, slots, lambda r, i: r.at[pl.ds(2 * i, 2)], *gs)
    gath.start()
    local = pltpu.make_async_copy(wo4, slots.at[t], lsem)
    local.start()
    scale = 1.0 / math.sqrt(HD)

    def attend(r):
        @pl.loop(0, 8)
        def _(i):
            h, sub = i // 2, i % 2
            rows = pl.ds(pl.multiple_of(r * 256 + sub * 128, 128), 128)
            s = lax.dot_general(
                qkv[h, rows, :], qkv[4 + h], (((1,), (1,)), ((), ())), preferred_element_type=F32
            )
            p = jnp.where(segc[rows, :] == segr[...], jnp.exp(s * scale), 0.0)
            total = jnp.sum(p, axis=-1, keepdims=True)
            o = jnp.dot(p.astype(BF), qkv[8 + h], preferred_element_type=F32) / total
            oh[h, pl.ds(pl.multiple_of(sub * 128, 128), 128), :] = o.astype(BF)

        att[x, pl.ds(r * 256, 256), :] = jnp.concatenate([oh[h][:, :HD] for h in range(4)], axis=1)

    rings = []
    for r in range(4):

        def part(s, i, r=r):
            return att.at[s, pl.ds(r * 256 + 128 * i, 128)]

        rings.append(
            RingGather(
                lambda i, part=part: part(x, i),
                part,
                lambda k, r=r: xs.at[r, k],
                lambda k, r=r: xr.at[r, k],
            )
        )
    attend(0)
    rings[0].start()
    gath.z_near()
    gath.z_far()
    attend(1)
    rings[1].start()
    rings[0].relay()
    gath.y_near(0)
    attend(2)
    rings[2].start()
    gath.y_near(1)
    attend(3)
    rings[3].start()
    rings[1].relay()
    gath.y_near(2)
    gath.y_near(3)
    rings[2].relay()
    for i in range(4):
        gath.y_far(i)
    rings[3].relay()
    local.wait()
    gath.wait_all()

    @pl.loop(0, 8)
    def _(g):
        for b in range(4):
            parts = [slots[4 * g + j, b] for j in range(4)]
            wof[b, pl.ds(pl.multiple_of(g * 208, 16), 208), :] = jnp.concatenate(parts, axis=0)

    for ring in rings:
        ring.wait_near()
        ring.wait_far()
        ring.finish()
    gath.finish()


class RingReduce:
    def __init__(self, sbuf, far_in, main_in, ss, rs, half):
        x = lax.axis_index("blk")
        self.hi, self.lo, self.far = (x + 1) % 4, (x + 3) % 4, (x + 2) % 4
        self.sbuf, self.far_in, self.main_in = sbuf, far_in, main_in
        right, left = x_dev(x, 1), x_dev(x, 3)
        self.a, self.b = pl.ds(0, half), pl.ds(half, half)
        a, b = self.a, self.b
        self.c = [
            rcopy(sbuf.at[self.far, a], far_in.at[0], ss(0), rs(0), right),
            rcopy(sbuf.at[self.far, b], far_in.at[1], ss(1), rs(1), left),
            rcopy(sbuf.at[self.hi, b], main_in.at[0, b], ss(2), rs(2), right),
            rcopy(sbuf.at[self.lo, a], main_in.at[1, a], ss(3), rs(3), left),
            rcopy(sbuf.at[self.hi, a], main_in.at[0, a], ss(4), rs(4), right),
            rcopy(sbuf.at[self.lo, b], main_in.at[1, b], ss(5), rs(5), left),
        ]

    def start(self):
        for k in range(4):
            self.c[k].start()

    def relay(self):
        self.c[0].wait_recv()
        s = self.sbuf[self.hi, self.a].astype(F32) + self.far_in[0].astype(F32)
        self.sbuf[self.hi, self.a] = s.astype(BF)
        self.c[1].wait_recv()
        s = self.sbuf[self.lo, self.b].astype(F32) + self.far_in[1].astype(F32)
        self.sbuf[self.lo, self.b] = s.astype(BF)
        self.c[4].start()
        self.c[5].start()

    def wait(self):
        for k in range(2, 6):
            self.c[k].wait_recv()

    def finish(self):
        for d in self.c:
            d.wait_send()


def gelu(v):
    return 0.5 * v * (1.0 + lax.erf(v * (1.0 / math.sqrt(2.0))))


def k_mlp(
    att, wof, toks, ob, gain, bias, fc1, b1, fc2, b2, wp, lo, wpg,
    w1, w2, after, h2, hid, part, own, sbuf, far_in, main_in, lsem, xs, xr, *gs
):
    x, y, z, c = position()
    t = lax.axis_index("tok")
    load = [
        pltpu.make_async_copy(fc1, w1, lsem.at[0]),
        pltpu.make_async_copy(fc2, w2, lsem.at[1]),
        pltpu.make_async_copy(wp, wpg.at[t], lsem.at[2]),
    ]
    for d in load:
        d.start()
    meet(x_peers() + tok_peers())
    gath = TokGather(wp, wpg, lambda r, i: r.at[pl.ds(96 * i, 96 + 16 * i)], *gs)
    gath.start()
    tiles = [(n, min(256, 1664 - n)) for n in range(0, 1664, 256)]

    def ring(r):
        return RingReduce(
            sbuf.at[r],
            far_in.at[r],
            main_in.at[r],
            lambda k: xs.at[r, k],
            lambda k: xr.at[r, k],
            128,
        )

    @pl.loop(0, 6)
    def _(r):
        @pl.when(r < 4)
        def _():
            rows = pl.ds(pl.multiple_of(r * 256, 256), 256)
            for n, w in tiles:
                acc = toks[r, :, n : n + w].astype(F32) + ob[:, n : n + w]
                for b in range(4):
                    acc += lax.dot_general(
                        att[b, rows, :],
                        wof[b, n : n + w, :],
                        (((1,), (1,)), ((), ())),
                        preferred_element_type=F32,
                    )
                after[:, n : n + w] = acc
            norm_rows(after, h2, gain, bias, 256)
            for j in range(4):

                @pl.when(x == j)
                def _():
                    own[r] = after[:, 416 * j : 416 * j + 416] + b2[...]

            @pl.when(r == 0)
            def _():
                load[0].wait()

            @pl.loop(0, 8)
            def _(j):
                cols = pl.ds(pl.multiple_of(j * 256, 256), 256)
                v = jnp.dot(h2[...], w1[:, cols], preferred_element_type=F32) + b1[:, cols]
                hid[:, cols] = gelu(v).astype(BF)

            @pl.when(r == 0)
            def _():
                load[1].wait()
                gath.z_near()
                gath.z_far()

            for n, w in tiles:
                part[:, n : n + w] = jnp.dot(hid[...], w2[:, n : n + w], preferred_element_type=F32)
            for j in range(4):
                piece = part[:, 416 * j : 416 * j + 416]
                sbuf[r, j] = piece.astype(BF)

                @pl.when(x == j)
                def _():
                    own[r] += piece

            @pl.when(r == 1)
            def _():
                gath.y_near(0)
                gath.y_near(1)

            @pl.when(r == 2)
            def _():
                gath.y_near(2)
                gath.y_near(3)

            ring(r).start()

        @pl.when((r > 0) & (r < 5))
        def _():
            ring(r - 1).relay()

        @pl.when(r > 1)
        def _():
            q = r - 2
            rg = ring(q)
            rg.wait()
            total = own[q] + main_in[q, 0].astype(F32) + main_in[q, 1].astype(F32)
            lo[pl.ds(pl.multiple_of(q * 256, 256), 256), :] = total.astype(BF)
            rg.finish()

        @pl.when(r == 3)
        def _():
            for i in range(4):
                gath.y_far(i)

    load[2].wait()
    gath.wait_all()
    gath.finish()


def k_proj(
    lo, gain, bias, mi, wpg, pb, out, fin, sbuf, own, far_in, main_in, st, ss, sr, xs, xr
):
    x, y, z, c = position()
    meet(x_peers() + [x_dev(x, 2)])
    n_loc = lo.shape[1]

    @pl.loop(0, 8)
    def _(i):
        rows = pl.ds(pl.multiple_of(i * 128, 128), 128)
        v = lo[rows, :].astype(F32)
        mean = jnp.mean(v, axis=-1, keepdims=True)
        d = v - mean
        m2 = jnp.sum(d * d, axis=-1, keepdims=True)
        lane = lax.broadcasted_iota(jnp.int32, (128, 128), 1)
        both = jnp.where(lane == 0, mean, jnp.where(lane == 1, m2, 0.0))
        st[x, :, rows] = both.T[:8]

    sends = [rcopy(st.at[x], st.at[x], ss.at[k], sr.at[k], x_dev(x, k + 1)) for k in range(3)]
    for d in sends:
        d.start()
    for d in sends:
        d.wait_recv()
    means = [st[s, 0:1, :] for s in range(4)]
    mean = 0.25 * (means[0] + means[1] + means[2] + means[3])
    m2 = st[0, 1:2, :] + st[1, 1:2, :] + st[2, 1:2, :] + st[3, 1:2, :]
    for s in range(4):
        d = means[s] - mean
        m2 = m2 + n_loc * (d * d)
    rstd = lax.rsqrt(m2 * (1.0 / (4 * n_loc)) + EPS)
    for i in range(8):
        sl = slice(128 * i, 128 * i + 128)
        row = lax.broadcasted_iota(jnp.int32, (128, 128), 0)
        cols = jnp.where(row == 0, mean[:, sl], jnp.where(row == 1, rstd[:, sl], 0.0)).T
        v = lo[sl, :].astype(F32)
        fin[sl, :] = ((v - cols[:, 0:1]) * cols[:, 1:2] * gain[...] + bias[...]).astype(BF)
    own[...] = jnp.zeros_like(own)

    @pl.loop(0, 4)
    def _(k):
        pick = (mi[k] == lax.broadcasted_iota(jnp.int32, (256, 1024), 1)).astype(BF)
        got = jnp.dot(pick, fin[...], preferred_element_type=F32).astype(BF)

        @pl.loop(0, 4)
        def _(j):
            own[j] += jnp.dot(got, wpg[k * 4 + j], preferred_element_type=F32)

    @pl.loop(0, 4)
    def _(j):
        sbuf[j] = own[j].astype(BF)

    rg = RingReduce(sbuf, far_in, main_in, lambda k: xs.at[k], lambda k: xr.at[k], 128)
    rg.start()
    rg.relay()
    rg.wait()
    total = own[x] + main_in[0].astype(F32) + main_in[1].astype(F32) + pb[...]
    out[...] = total.astype(BF)
    rg.finish()
    for d in sends:
        d.wait_send()


def kernel_call(body, name, cid, ins, outs, scratch, args):
    return pl.pallas_call(
        body,
        name=name,
        out_shape=outs,
        in_specs=ins,
        out_specs=[VM] * len(outs),
        scratch_shapes=scratch,
        compiler_params=pltpu.CompilerParams(
            collective_id=cid, has_side_effects=True, vmem_limit_bytes=VLIM
        ),
    )(*args)


def sds(shape, dtype):
    return jax.ShapeDtypeStruct(shape, dtype)


DMA = pltpu.SemaphoreType.DMA


def body(
    tokens,
    segment_ids,
    merge_index,
    segment_owner,
    ln1_gain,
    ln1_bias,
    w_qkv,
    qkv_bias,
    w_out,
    out_bias,
    ln2_gain,
    ln2_bias,
    w_fc1,
    fc1_bias,
    w_fc2,
    fc2_bias,
    ln3_gain,
    ln3_bias,
    w_proj,
    proj_bias,
):
    x = lax.axis_index("blk")
    tok = tokens[0]
    width = tok.shape[1]
    part_w = w_qkv.shape[2]
    depth = w_qkv.shape[1]
    heads = part_w // HD
    cols = 3 * heads * HPAD
    pad = ((0, 0), (0, 0), (0, 0), (0, HPAD - HD))
    wl = jnp.pad(w_qkv.transpose(1, 0, 2).reshape(depth, 3, heads, HD), pad).reshape(depth, cols)
    qb = jnp.pad(qkv_bias.reshape(1, 3, heads, HD), pad).reshape(1, cols)
    wo = w_out.T
    perm = []
    for bx in range(4):
        for t in range(32):
            ty, tz, tc = t // 8, (t // 2) % 4, t % 2
            perm.append((bx * 32 + t, tz * 32 + (ty * 4 + bx) * 2 + tc))
    wp = lax.ppermute(w_proj, ("blk", "tok"), perm)

    def row(v):
        return v.reshape(1, -1)

    toks, qkv, wo4 = kernel_call(
        k_qkv,
        "qkv",
        1,
        [VM] * 6,
        [sds((4, 256, width), BF), sds((3 * heads, 1024, HPAD), BF), sds((4, depth, part_w), BF)],
        [
            pltpu.VMEM((32, depth, cols), BF),
            pltpu.VMEM((width, cols), BF),
            pltpu.VMEM((4, 256, width), BF),
            DMA((3,)),
            DMA((6,)),
            DMA((6,)),
            DMA((3,)),
            DMA((3,)),
        ]
        + TOK_SEMS,
        (tok, wl, wo, row(ln1_gain), row(ln1_bias), qb),
    )
    seg = segment_ids[0]
    att, wof = kernel_call(
        k_att,
        "attention",
        2,
        [VM] * 4,
        [sds((4, 1024, part_w), BF), sds((4, width, part_w), BF)],
        [
            pltpu.VMEM((heads, 256, HPAD), BF),
            pltpu.VMEM((32, 4, depth, part_w), BF),
            DMA,
            DMA((4, 6)),
            DMA((4, 6)),
        ]
        + TOK_SEMS,
        (qkv, seg.reshape(-1, 1), seg.reshape(1, -1), wo4),
    )
    hidden = w_fc1.shape[1]

    def mine(v):
        return lax.dynamic_slice_in_dim(v, x * part_w, part_w, 0).reshape(1, -1)

    lo, wpg = kernel_call(
        k_mlp,
        "mlp",
        3,
        [VM, VM, VM, VM, VM, VM, ANY, VM, ANY, VM, VM],
        [sds((1024, part_w), BF), sds((32, 208, part_w), BF)],
        [
            pltpu.VMEM((width, hidden), BF),
            pltpu.VMEM((hidden, width), BF),
            pltpu.VMEM((256, width), F32),
            pltpu.VMEM((256, width), BF),
            pltpu.VMEM((256, hidden), BF),
            pltpu.VMEM((256, width), F32),
            pltpu.VMEM((4, 256, part_w), F32),
            pltpu.VMEM((4, 4, 256, part_w), BF),
            pltpu.VMEM((4, 2, 128, part_w), BF),
            pltpu.VMEM((4, 2, 256, part_w), BF),
            DMA((3,)),
            DMA((4, 6)),
            DMA((4, 6)),
        ]
        + TOK_SEMS,
        (
            att, wof, toks, row(out_bias), row(ln2_gain), row(ln2_bias),
            w_fc1, row(fc1_bias), w_fc2, mine(fc2_bias), wp,
        ),
    )
    merge_rows = merge_index[0]
    merged_count = merge_rows.shape[0]
    projected = kernel_call(
        k_proj,
        "merge",
        4,
        [VM] * 6,
        [sds((merged_count, part_w), BF)],
        [
            pltpu.VMEM((1024, part_w), BF),
            pltpu.VMEM((4, 256, part_w), BF),
            pltpu.VMEM((4, 256, part_w), F32),
            pltpu.VMEM((2, 128, part_w), BF),
            pltpu.VMEM((2, 256, part_w), BF),
            pltpu.VMEM((4, 8, 1024), F32),
            DMA((3,)),
            DMA((3,)),
            DMA((6,)),
            DMA((6,)),
        ],
        (
            lo,
            mine(ln3_gain),
            mine(ln3_bias),
            merge_rows.T.reshape(4, merged_count, 1),
            wpg.reshape(16, part_w, part_w),
            row(proj_bias),
        ),
    )[0]
    tok_count = lax.axis_size("tok")
    slot_cap = 2 * merged_count // tok_count
    owners_here = segment_owner[0]
    seg_rows = jnp.take(seg, merge_rows[:, 0])
    seg_match = (
        seg_rows[:, None] == jnp.arange(owners_here.shape[0], dtype=jnp.int32)[None, :]
    ).astype(jnp.int32)
    owner_rows = jnp.sum(seg_match * owners_here[None, :], axis=1)
    segment_matches = (
        owner_rows[:, None] == jnp.arange(tok_count, dtype=jnp.int32)[None, :]
    ).astype(jnp.int32)
    before = jnp.cumsum(segment_matches, axis=0) - segment_matches
    order_in = jnp.sum(before * segment_matches, axis=1)
    target = owner_rows * slot_cap + order_in
    placed = (jnp.arange(tok_count * slot_cap, dtype=jnp.int32)[:, None] == target[None, :]).astype(BF)
    outgoing = jnp.dot(placed, projected, preferred_element_type=F32).astype(BF)
    outgoing = outgoing.reshape(tok_count, slot_cap, projected.shape[1])
    arrived = lax.all_to_all(outgoing, "tok", split_axis=0, concat_axis=0, tiled=True)
    return arrived[None]


def solution(mesh):
    placed = (
        P("tok", "blk", None),
        P("tok", None),
        P("tok", None, None),
        P("tok", None),
        P(),
        P(),
        P(None, "tok", "blk"),
        P(None, "blk"),
        P("blk", "tok"),
        P(),
        P(),
        P(),
        P(None, "blk"),
        P("blk"),
        P("blk", None),
        P(),
        P(),
        P(),
        P("tok", "blk"),
        P("blk"),
    )
    return jax.shard_map(
        body, mesh=mesh, in_specs=placed, out_specs=P("tok", None, None, "blk"), check_vma=False
    )
```

time: 490 us -> 254 us (0.52); the launches traced: 481 us -> 253 us
  waiting for transfers between devices: 322 us -> 0.01 us
  Pallas kernels: 0 us -> 205 us
  matrix products: 73 us -> 1.3 us
  other arithmetic: 24.6 us -> 2.87 us
  between operations: 14 us -> 0.11 us
  local copies, waits for them, and re-layouts: 30.3 us -> 21.1 us
    all_gather x5 -> x0, waiting for transfers between devices: 208 us -> none  [the longest x1 53.1 us: body(): lax.all_gather(w_qkv, 'tok', axis=1, tiled=True)]
    pallas_call x0 -> x4, Pallas kernels: none -> 205 us  [kernel_call(): pl.pallas_call(body, name=name, out_shape=outs, in_specs=ins, out_specs=[...]
    psum x1 -> x0, waiting for transfers between devices: 73.7 us -> none  [body(): lax.psum(partial_sum.astype(jnp.bfloat16), 'blk').astype(jnp.float32)]
    dot_general x9 -> x1, matrix products: 73 us -> 1.3 us  [body(): outgoing = jnp.dot(placed, projected, preferred_element_type=F32).astype(BF)]
    reduce_scatter x1 -> x0, waiting for transfers between devices: 38.9 us -> none  [body(): lax.psum_scatter(jnp.dot(attended, out_full, preferred_element_type=jnp.f...]
    reduce_sum x6 -> x0, other arithmetic: 12.1 us -> none  [the longest x3 6.36 us: layer_norm(): spread = jnp.mean(center * center, axis=-1, keepdims=True)]
    reshape x0 -> x10, local copies, waits for them, and re-layouts: none -> 10.9 us  [the longest x5 6.46 us: row(): return v.reshape(1, -1)]
    gather x3 -> x1, local copies, waits for them, and re-layouts: 12.7 us -> 1.92 us  [body(): seg_rows = jnp.take(seg, merge_rows[:, 0])]
  transfers between devices with their start and end apart: 7 -> 1, of which waited for: 7 -> 0; matrix products, arithmetic and copies ran while one was open for 8% -> 9% of each run, Pallas kernels for 0% -> 43%
where the time goes in v1:
time: 254 us; the launch traced here: 253 us
  Pallas kernels  205 us (81%)
  local copies, waits for them, and re-layouts  21.1 us (8%)
  blocking collectives  20.4 us (8%)
  other arithmetic  2.87 us (1%)
    pallas_call x4, Pallas kernels, kernel_call(): pl.pallas_call(body, name=name, out_shape=outs, in_specs=ins, out_specs=[...  205 us
    all_to_all x1, blocking collectives, body(): lax.all_to_all(outgoing, 'tok', split_axis=0, concat_axis=0, tiled=True)  20.4 us
    reshape x5, local copies, waits for them, and re-layouts, row(): return v.reshape(1, -1)  6.46 us
  transfers between devices with their start and end apart: 1, of which 0 were waited for; matrix products, arithmetic and copies ran while one was open for 9% of the time, Pallas kernels for 43%

profile of v1, /device:TPU:1, one launch (start us, length us, event | category | flops | bytes accessed | tf_op | source)
XLA Modules:
  0.0 252.7 jit_solution(683705695895881176)
XLA Ops:
  0.0 1.6 collective-permute-start
  1.6 1.1 reshape.79
  2.7 0.1 copy.24
  2.7 0.1 pad.8
  2.8 0.7 reshape.80.wl
  3.6 0.8 reshape.83
  4.3 1.3 reshape.81.gain
  5.6 1.3 reshape.82.bias
  6.9 1.7 copy.25.segc
  8.6 1.3 reshape.85.ob
  9.9 1.3 reshape.86.gain
  11.2 1.3 reshape.87.bias
  12.5 1.3 dynamic_slice.9
  13.8 1.4 dynamic_slice.10
  15.2 1.4 dynamic_slice.11
  16.6 1.7 copy.26.mi
  18.3 0.7 compare_select_fusion
  19.0 1.9 gather_fusion
  20.9 0.7 and_select_fusion
  21.6 0.7 select_reduce_fusion
  22.4 0.6 reduce-window.6
  23.0 0.2 slice_reduce_fusion
  23.2 0.1 fusion.3
  23.3 0.6 pad.9
  23.9 54.6 %qkv.1 = (bf16[4,256,1664]{2,1,0:T(8,128)(2,1)}, bf16[12,1024,128]{2,1,0:T(8,128)(2,1)}, bf16[4,52,416]{2,1,0:T(8,128)(2,1)}) custom-call(bf16[256,1664]{1,0:T(8,128)(2,1)} %bitcast.51, bf16[52,1536]{1,0:T(8,128)(2,1)} %reshape.80.wl, bf16[52,416]{1,0:T(8,128)(2,1)} %bitcast.53, f32[1,1664]{1,0:T(1,128)} %reshape.81.gain, f32[1,1664]{1,0:T(1,128)} %reshape.82.bias, ...), custom_call_target="tpu_custom_call" | custom-call | tf_op jit(solution)/shard_map/qkv/pallas_call | solution.py:577
  78.5 53.3 %attention.1 = (bf16[4,1024,416]{2,1,0:T(8,128)(2,1)}, bf16[4,1664,416]{2,1,0:T(8,128)(2,1)}) custom-call(bf16[12,1024,128]{2,1,0:T(8,128)(2,1)} %get-tuple-element.12.qkv, s32[1024,1]{1,0:T(8,128)} %copy.25.segc, s32[1,1024]{1,0:T(1,128)} %segr.1, bf16[4,52,416]{2,1,0:T(8,128)(2,1)} %get-tuple-element.13.wo4), custom_call_target="tpu_custom_call" | custom-call | tf_op jit(solution)/shard_map/attention/pallas_call | solution.py:577
  131.8 0.0 collective-permute-done.wp
  131.8 0.0 copy-start
  131.8 0.7 copy-done
  132.5 69.5 %mlp.1 = (bf16[1024,416]{1,0:T(8,128)(2,1)}, bf16[32,208,416]{2,1,0:T(8,128)(2,1)}) custom-call(bf16[4,1024,416]{2,1,0:T(8,128)(2,1)} %get-tuple-element.14.att, bf16[4,1664,416]{2,1,0:T(8,128)(2,1)} %get-tuple-element.15.wof, bf16[4,256,1664]{2,1,0:T(8,128)(2,1)} %get-tuple-element.16.toks, f32[1,1664]{1,0:T(1,128)} %reshape.85.ob, ...), custom_call_target="tpu_custom_call" | custom-call | tf_op jit(solution)/shard_map/mlp/pallas_call | solution.py:577
  202.0 28.0 %merge.1 = bf16[256,416]{1,0:T(8,128)(2,1)} custom-call(bf16[1024,416]{1,0:T(8,128)(2,1)} %get-tuple-element.17.lo, f32[1,416]{1,0:T(1,128)} %bitcast.60, f32[1,416]{1,0:T(1,128)} %bitcast.61, s32[4,256,1]{2,1,0:T(8,128)} %copy.26.mi, bf16[16,416,416]{2,1,0:T(8,128)(2,1)} %bitcast.48, f32[1,416]{1,0:T(1,128)} %bitcast.66), custom_call_target="tpu_custom_call" | custom-call | tf_op jit(solution)/shard_map/merge/pallas_call | solution.py:577
  230.1 1.3 convolution_convert_fusion
  231.4 0.2 copy.27
  231.6 20.4 %all_to_all.5 = bf16[32,16,416]{2,1,0:T(8,128)(2,1)S(1)} all-to-all(bf16[32,16,416]{2,1,0:T(8,128)(2,1)S(1)} %bitcast.49), channel_id=1, replica_groups=mesh['blk'=4,'tok'=32] {'tok'}, dimensions={0} | all-to-all | bytes 851968 | tf_op jit(solution)/shard_map/all_to_all | solution.py:754
  251.9 0.8 copy.31
  (5 shorter events, 0.1 us)
Async XLA Ops:
  0.0 131.8 %collective-permute-start = (bf16[208,416]{1,0:T(8,128)(2,1)}, bf16[208,416]{1,0:T(8,128)(2,1)S(1)}, u32[]{:S(2)}, u32[]{:S(2)}) collective-permute-start(bf16[208,416]{1,0:T(8,128)(2,1)} %param.38), channel_id=1, source_target_pairs={{0,0},{1,1},{2,32},{3,33},{4,64},{5,65},{6,96},{7,97},{8,8},{9,9},... | collective-permute-start | bytes 519176 | tf_op jit(solution)/shard_map/ppermute | solution.py:635
  131.8 0.7 copy-start

commit v2 on v1

v2 whole, which is shorter than its diff:
```python
import math

import jax
import jax.numpy as jnp
from jax import lax
from jax.experimental import pallas as pl
from jax.experimental.pallas import tpu as pltpu
from jax.sharding import PartitionSpec as P

HD = 104
HPAD = 128
EPS = 1e-06
BF = jnp.bfloat16
F32 = jnp.float32
MESH_ID = pl.DeviceIdType.MESH
VLIM = 65000 * 1024
VM = pl.BlockSpec(memory_space=pltpu.VMEM)
ANY = pl.BlockSpec(memory_space=pl.ANY)


def position():
    x = lax.axis_index("blk")
    t = lax.axis_index("tok")
    return x, t // 8, (t // 2) % 4, t % 2


def tok_of(y, z, c):
    return ((y % 4) * 4 + z % 4) * 2 + c


def rcopy(src, dst, ssem, rsem, dev):
    return pltpu.make_async_remote_copy(
        src_ref=src, dst_ref=dst, send_sem=ssem, recv_sem=rsem, device_id=dev, device_id_type=MESH_ID
    )


def x_dev(x, off):
    return {"blk": (x + off) % 4}


def meet(peers):
    bar = pltpu.get_barrier_semaphore()
    for dev in peers:
        pl.semaphore_signal(bar, inc=1, device_id=dev, device_id_type=MESH_ID)
    pl.semaphore_wait(bar, len(peers))


def x_peers():
    x, y, z, c = position()
    return [x_dev(x, 1), x_dev(x, 3)]


def tok_peers():
    x, y, z, c = position()
    return [
        {"tok": tok_of(y, z + 1, c)},
        {"tok": tok_of(y, z + 3, c)},
        {"tok": tok_of(y + 1, z, c)},
        {"tok": tok_of(y + 3, z, c)},
        {"tok": tok_of(y, z, 1 - c)},
    ]


class RingGather:
    def __init__(self, own, half, ss, rs):
        x = lax.axis_index("blk")
        right, left = x_dev(x, 1), x_dev(x, 3)

        def send(view, src, i, k, dev):
            return rcopy(view, half(src, i), ss(k), rs(k), dev)

        me, lo, hi = x, (x + 3) % 4, (x + 1) % 4
        self.c = [
            send(own(0), me, 0, 0, right),
            send(own(1), me, 1, 1, right),
            send(own(1), me, 1, 2, left),
            send(own(0), me, 0, 3, left),
            send(half(lo, 0), lo, 0, 4, right),
            send(half(hi, 1), hi, 1, 5, left),
        ]

    def start(self):
        for k in (0, 2, 1, 3):
            self.c[k].start()

    def relay(self):
        self.c[0].wait_recv()
        self.c[4].start()
        self.c[2].wait_recv()
        self.c[5].start()

    def wait_near(self):
        self.c[1].wait_recv()
        self.c[3].wait_recv()

    def wait_far(self):
        self.c[4].wait_recv()
        self.c[5].wait_recv()

    def finish(self):
        for c in self.c:
            c.wait_send()


class TokGather:
    OFF = (0, 3, 1, 2)

    def __init__(self, own, slots, view, fs, fr, ss, sr, cs, cr):
        x, y, z, c = position()
        self.first, self.second, self.cross = [], [], []
        sib = {"tok": tok_of(y, z, 1 - c)}
        for h in range(2):

            def tok(d1, d2, h=h):
                return tok_of(y + d2, z + d1, c) if h == 0 else tok_of(y + d1, z + d2, c)

            def slot(d1, d2, tok=tok):
                return slots.at[tok(d1, d2)]

            def half(r, h=h):
                return view(r, h, None)

            def quarter(r, q, h=h):
                return view(r, h, q)

            me = slot(0, 0)
            p1, m1 = {"tok": tok(1, 0)}, {"tok": tok(3, 0)}
            p2, m2 = {"tok": tok(0, 1)}, {"tok": tok(0, 3)}
            self.first.append(
                [
                    rcopy(half(own), half(me), fs.at[h, 0], fr.at[h, 0], p1),
                    rcopy(half(own), half(me), fs.at[h, 1], fr.at[h, 1], m1),
                    rcopy(quarter(slot(3, 0), 0), quarter(slot(3, 0), 0), fs.at[h, 2], fr.at[h, 2], p1),
                    rcopy(quarter(slot(1, 0), 1), quarter(slot(1, 0), 1), fs.at[h, 3], fr.at[h, 3], m1),
                ]
            )
            second = []
            for i, o in enumerate(self.OFF):
                src = half(own) if i == 0 else half(slot(o, 0))
                here, up, dn = half(slot(o, 0)), slot(o, 3), slot(o, 1)
                second.append(
                    [
                        rcopy(src, here, ss.at[h, i, 0], sr.at[h, i, 0], p2),
                        rcopy(src, here, ss.at[h, i, 1], sr.at[h, i, 1], m2),
                        rcopy(quarter(up, 0), quarter(up, 0), ss.at[h, i, 2], sr.at[h, i, 2], p2),
                        rcopy(quarter(dn, 1), quarter(dn, 1), ss.at[h, i, 3], sr.at[h, i, 3], m2),
                    ]
                )
            self.second.append(second)
            cross = []
            for k in range(4):
                row = []
                for i, o in enumerate(self.OFF):
                    dst = half(slot(o, self.OFF[k]))
                    src = half(own) if (i == 0 and k == 0) else dst
                    row.append(rcopy(src, dst, cs.at[h, k, i], cr.at[h, k, i], sib))
                cross.append(row)
            self.cross.append(cross)

    def start(self):
        for h in range(2):
            self.first[h][0].start()
            self.first[h][1].start()
        for h in range(2):
            self._fan(h, 0)

    def _fan(self, h, i):
        self.second[h][i][0].start()
        self.second[h][i][1].start()
        self.cross[h][0][i].start()

    def first_near(self):
        for h in range(2):
            f = self.first[h]
            f[0].wait_recv()
            f[2].start()
            self._fan(h, 1)
            f[1].wait_recv()
            f[3].start()
            self._fan(h, 2)

    def first_far(self):
        for h in range(2):
            self.first[h][2].wait_recv()
            self.first[h][3].wait_recv()
            self._fan(h, 3)

    def second_near(self, i):
        for h in range(2):
            f = self.second[h][i]
            f[0].wait_recv()
            f[2].start()
            self.cross[h][1][i].start()
            f[1].wait_recv()
            f[3].start()
            self.cross[h][2][i].start()

    def second_far(self, i):
        for h in range(2):
            f = self.second[h][i]
            f[2].wait_recv()
            f[3].wait_recv()
            self.cross[h][3][i].start()

    def _all(self):
        for h in range(2):
            for row in self.cross[h]:
                yield from row

    def wait_all(self):
        for d in self._all():
            d.wait_recv()

    def finish(self):
        for h in range(2):
            for d in self.first[h]:
                d.wait_send()
            for row in self.second[h]:
                for d in row:
                    d.wait_send()
        for d in self._all():
            d.wait_send()


TOK_SEMS = [pltpu.SemaphoreType.DMA((2, 4))] * 2 + [pltpu.SemaphoreType.DMA((2, 4, 4))] * 4


def norm_rows(src, dst, gain, bias, rows, step=32):
    @pl.loop(0, rows // step)
    def _(i):
        at = pl.ds(pl.multiple_of(i * step, step), step)
        v = src[at, :].astype(F32)
        mean = jnp.mean(v, axis=-1, keepdims=True)
        center = v - mean
        spread = jnp.mean(center * center, axis=-1, keepdims=True)
        dst[at, :] = (center * lax.rsqrt(spread + EPS) * gain[...] + bias[...]).astype(dst.dtype)


def view_cols(r, h, q):
    return r.at[:, pl.ds(768 * h, 768)] if q is None else r.at[:, pl.ds(768 * h + 384 * q, 384)]


def view_lead(r, h, q):
    return r.at[pl.ds(2 * h, 2)] if q is None else r.at[pl.ds(2 * h + q, 1)]


def view_rows(r, h, q):
    start, size = ((0, 112), (112, 96))[h]
    if q is None:
        return r.at[pl.ds(start, size)]
    first = (64, 48)[h]
    return r.at[pl.ds(start, first)] if q == 0 else r.at[pl.ds(start + first, size - first)]


def k_qkv(
    tok, wq, wout, gain, bias, qbias, toks_o, qkv_o, wof_o,
    wl, qb, wo4, toks, qkv, slots, wslots, wf, wof, hb, lsem, osem, xs, xr, ws, wr, *gs
):
    x, y, z, c = position()
    t = lax.axis_index("tok")
    depth = wq.shape[1]
    heads = wq.shape[2] // HD
    meet(x_peers() + [x_dev(x, 2)] + tok_peers())
    ring = RingGather(
        lambda i: tok.at[pl.ds(128 * i, 128)],
        lambda s, i: toks.at[s, pl.ds(128 * i, 128)],
        lambda k: xs.at[k],
        lambda k: xr.at[k],
    )
    ring.start()
    zero = jnp.zeros((depth, HPAD - HD), BF)
    for k in range(3):
        for h in range(heads):
            at = (k * heads + h) * HPAD
            wl[:, at : at + HPAD] = jnp.concatenate([wq[k, :, h * HD : h * HD + HD], zero], axis=1)
            qb[:, at : at + HPAD] = jnp.concatenate(
                [qbias[k : k + 1, h * HD : h * HD + HD], jnp.zeros((1, HPAD - HD), F32)], axis=1
            )
    wo4[x] = wout[...].T
    gq = TokGather(wl, slots, view_cols, *gs[:6])
    go = TokGather(wo4, wslots, view_lead, *gs[6:])
    gq.start()
    wo_send = [rcopy(wo4.at[x], wo4.at[x], ws.at[k], wr.at[k], x_dev(x, k + 1)) for k in range(3)]
    for d in wo_send:
        d.start()
    local = [
        pltpu.make_async_copy(tok, toks.at[x], lsem.at[0]),
        pltpu.make_async_copy(wl, slots.at[t], lsem.at[1]),
    ]
    for d in local:
        d.start()
    norm_rows(tok, hb.at[x], gain, bias, 256)
    gq.first_near()
    for d in wo_send:
        d.wait_recv()
    go.start()
    local.append(pltpu.make_async_copy(wo4, wslots.at[t], lsem.at[2]))
    local[2].start()
    gq.first_far()
    gq.second_near(0)
    ring.relay()
    for i in range(1, 4):
        gq.second_near(i)
    go.first_near()
    go.first_far()
    ring.wait_near()
    local[0].wait()
    outs = []

    def put(src, dst):
        outs.append(pltpu.make_async_copy(src, dst, osem.at[len(outs)]))
        outs[-1].start()

    for o in (0, 1, 3):
        s = (x + o) % 4
        put(toks.at[s], toks_o.at[s])
        if o:
            norm_rows(toks.at[s], hb.at[s], gain, bias, 256)
    for i in range(4):
        gq.second_far(i)
    for i in range(4):
        go.second_near(i)
    local[1].wait()
    gq.wait_all()

    @pl.loop(0, 8)
    def _(g):
        parts = [slots[4 * g + j] for j in range(4)]
        wf[pl.ds(pl.multiple_of(g * 208, 16), 208), :] = jnp.concatenate(parts, axis=0)

    def project(s):
        @pl.loop(0, wf.shape[1] // 256)
        def _(j):
            cols = pl.ds(pl.multiple_of(j * 256, 256), 256)
            v = jnp.dot(hb[s], wf[:, cols], preferred_element_type=F32) + qb[:, cols]
            v = v.astype(BF)
            rows = pl.ds(pl.multiple_of(s * 256, 256), 256)
            qkv[2 * j, rows, :] = v[:, :128]
            qkv[2 * j + 1, rows, :] = v[:, 128:]

    @pl.loop(0, 3)
    def _(i):
        project((x + i + i // 2) % 4)

    for i in range(4):
        go.second_far(i)
    local[2].wait()
    go.wait_all()

    @pl.loop(0, 8)
    def _(g):
        for b in range(4):
            parts = [wslots[4 * g + j, b] for j in range(4)]
            wof[b, pl.ds(pl.multiple_of(g * 208, 16), 208), :] = jnp.concatenate(parts, axis=0)

    put(wof, wof_o)
    ring.wait_far()
    far = (x + 2) % 4
    put(toks.at[far], toks_o.at[far])
    norm_rows(toks.at[far], hb.at[far], gain, bias, 256)
    project(far)
    put(qkv, qkv_o)
    for d in wo_send:
        d.wait_send()
    ring.finish()
    gq.finish()
    go.finish()
    for d in outs:
        d.wait()


class RingReduce:
    def __init__(self, sbuf, far_in, main_in, ss, rs, half):
        x = lax.axis_index("blk")
        self.hi, self.lo, self.far = (x + 1) % 4, (x + 3) % 4, (x + 2) % 4
        self.sbuf, self.far_in, self.main_in = sbuf, far_in, main_in
        right, left = x_dev(x, 1), x_dev(x, 3)
        self.a, self.b = pl.ds(0, half), pl.ds(half, half)
        a, b = self.a, self.b
        self.c = [
            rcopy(sbuf.at[self.far, a], far_in.at[0], ss(0), rs(0), right),
            rcopy(sbuf.at[self.far, b], far_in.at[1], ss(1), rs(1), left),
            rcopy(sbuf.at[self.hi, b], main_in.at[0, b], ss(2), rs(2), right),
            rcopy(sbuf.at[self.lo, a], main_in.at[1, a], ss(3), rs(3), left),
            rcopy(sbuf.at[self.hi, a], main_in.at[0, a], ss(4), rs(4), right),
            rcopy(sbuf.at[self.lo, b], main_in.at[1, b], ss(5), rs(5), left),
        ]

    def start(self):
        for k in range(4):
            self.c[k].start()

    def relay(self):
        self.c[0].wait_recv()
        s = self.sbuf[self.hi, self.a].astype(F32) + self.far_in[0].astype(F32)
        self.sbuf[self.hi, self.a] = s.astype(BF)
        self.c[1].wait_recv()
        s = self.sbuf[self.lo, self.b].astype(F32) + self.far_in[1].astype(F32)
        self.sbuf[self.lo, self.b] = s.astype(BF)
        self.c[4].start()
        self.c[5].start()

    def wait(self):
        for k in range(2, 6):
            self.c[k].wait_recv()

    def finish(self):
        for d in self.c:
            d.wait_send()


def gelu(v):
    return 0.5 * v * (1.0 + lax.erf(v * (1.0 / math.sqrt(2.0))))


def k_layer(
    qkv, seg, toks_h, wof_h, ob, gain, bias, fc1, b1, fc2, b2, wp, lo, wpg,
    toks, wof, w1, w2, att, oh, segc, after, h2, hid, own, sbuf, far_in, main_in,
    lsem, as_, ar, xs, xr, *gs
):
    x, y, z, c = position()
    t = lax.axis_index("tok")
    load = [
        pltpu.make_async_copy(wof_h, wof, lsem.at[0]),
        pltpu.make_async_copy(toks_h, toks, lsem.at[1]),
        pltpu.make_async_copy(fc1, w1, lsem.at[2]),
        pltpu.make_async_copy(fc2, w2, lsem.at[3]),
        pltpu.make_async_copy(wp, wpg.at[t], lsem.at[4]),
    ]
    for d in load:
        d.start()
    segr = seg[...].astype(F32)
    segc[...] = jnp.broadcast_to(segr, (128, segr.shape[1])).T
    meet(x_peers() + tok_peers())
    gath = TokGather(wp, wpg, view_rows, *gs)
    gath.start()
    scale = 1.0 / math.sqrt(HD)
    heads = qkv.shape[0] // 3

    def attend(r):
        @pl.loop(0, 2)
        def _(sub):
            rows = pl.ds(pl.multiple_of(r * 256 + sub * 128, 128), 128)
            same = segc[rows, 0:1] == segr
            for h in range(heads):
                s = lax.dot_general(
                    qkv[h, rows, :], qkv[heads + h], (((1,), (1,)), ((), ())), preferred_element_type=F32
                )
                p = jnp.where(same, jnp.exp(s * scale), 0.0)
                total = jnp.sum(p, axis=-1, keepdims=True)
                o = jnp.dot(p.astype(BF), qkv[2 * heads + h], preferred_element_type=F32) / total
                oh[h, pl.ds(pl.multiple_of(sub * 128, 128), 128), :] = o.astype(BF)

        att[x, pl.ds(r * 256, 256), :] = jnp.concatenate([oh[h][:, :HD] for h in range(heads)], axis=1)

    def gather_ring(r):
        def part(s, i):
            return att.at[s, pl.ds(pl.multiple_of(r * 256 + 128 * i, 128), 128)]

        return RingGather(lambda i: part(x, i), part, lambda k: as_.at[r, k], lambda k: ar.at[r, k])

    def reduce_ring(r):
        return RingReduce(
            sbuf.at[r],
            far_in.at[r],
            main_in.at[r],
            lambda k: xs.at[r, k],
            lambda k: xr.at[r, k],
            128,
        )

    attend(0)
    gather_ring(0).start()
    gath.first_near()
    gath.first_far()
    attend(1)
    gather_ring(1).start()
    gather_ring(0).relay()
    attend(2)
    gather_ring(2).start()
    for i in range(4):
        gath.second_near(i)
    gather_ring(1).relay()
    attend(3)
    gather_ring(3).start()
    gather_ring(2).relay()
    for i in range(4):
        gath.second_far(i)
    tiles = [(n, min(256, 1664 - n)) for n in range(0, 1664, 256)]
    for d in load[:2]:
        d.wait()

    @pl.loop(0, 6)
    def _(r):
        @pl.when(r < 4)
        def _():
            rg = gather_ring(r)
            rg.wait_near()
            rg.wait_far()
            rows = pl.ds(pl.multiple_of(r * 256, 256), 256)
            for n, w in tiles:
                acc = toks[r, :, n : n + w].astype(F32) + ob[n : n + w]
                for b in range(4):
                    acc += lax.dot_general(
                        att[b, rows, :],
                        wof[b, n : n + w, :],
                        (((1,), (1,)), ((), ())),
                        preferred_element_type=F32,
                    )
                after[:, n : n + w] = acc

            @pl.when(r == 0)
            def _():
                gather_ring(3).relay()
                load[2].wait()

            @pl.when(r > 0)
            def _():
                reduce_ring(r - 1).relay()

            norm_rows(after, h2, gain, bias, 256)
            for j in range(4):

                @pl.when(x == j)
                def _():
                    own[r] = after[:, 416 * j : 416 * j + 416] + b2[416 * j : 416 * j + 416]

            for j in range(8):
                cols = slice(256 * j, 256 * j + 256)
                v = jnp.dot(h2[...], w1[:, cols], preferred_element_type=F32) + b1[cols]
                hid[:, cols] = gelu(v).astype(BF)

            @pl.when(r == 0)
            def _():
                load[3].wait()

            for n, w in tiles:
                after[:, n : n + w] = jnp.dot(hid[...], w2[:, n : n + w], preferred_element_type=F32)
            for j in range(4):
                piece = after[:, 416 * j : 416 * j + 416]
                sbuf[r, j] = piece.astype(BF)

                @pl.when(x == j)
                def _():
                    own[r] += piece

            reduce_ring(r).start()

        @pl.when(r == 4)
        def _():
            reduce_ring(3).relay()

        @pl.when(r > 1)
        def _():
            q = r - 2
            rg = reduce_ring(q)
            rg.wait()
            total = own[q] + main_in[q, 0].astype(F32) + main_in[q, 1].astype(F32)
            lo[pl.ds(pl.multiple_of(q * 256, 256), 256), :] = total.astype(BF)
            rg.finish()
            gather_ring(q).finish()

    load[4].wait()
    gath.wait_all()
    gath.finish()


def column(rows):
    n, m = rows.shape
    return jnp.concatenate([rows, jnp.zeros((128 - n, m), F32)], axis=0).T


def k_merge(
    lo, gain3, bias3, mi, seg, owners, wpg_h, pb, out,
    wpg, fin, gb, sbuf, own, far_in, main_in, st, placed, obuf, lsem, ss, sr, xs, xr, ts, tr
):
    x, y, z, c = position()
    t = lax.axis_index("tok")
    n_tok = out.shape[0]
    slot = out.shape[1]
    merged = mi.shape[1]
    n_loc = lo.shape[1]
    load = pltpu.make_async_copy(wpg_h, wpg, lsem.at[0])
    load.start()
    bar = pltpu.get_barrier_semaphore()

    @pl.loop(1, n_tok)
    def _(i):
        pl.semaphore_signal(bar, inc=1, device_id={"tok": (t + i) % n_tok}, device_id_type=MESH_ID)

    @pl.loop(1, 4)
    def _(i):
        pl.semaphore_signal(bar, inc=1, device_id=x_dev(x, i), device_id_type=MESH_ID)

    @pl.loop(0, 8)
    def _(i):
        rows = pl.ds(pl.multiple_of(i * 128, 128), 128)
        v = lo[rows, :].astype(F32)
        mean = jnp.mean(v, axis=-1, keepdims=True)
        d = v - mean
        m2 = jnp.sum(d * d, axis=-1, keepdims=True)
        lane = lax.broadcasted_iota(jnp.int32, (128, 128), 1)
        both = jnp.where(lane == 0, mean, jnp.where(lane == 1, m2, 0.0))
        st[x, :, rows] = both.T[:8]

    pl.semaphore_wait(bar, n_tok + 2)
    sends = [rcopy(st.at[x], st.at[x], ss.at[k], sr.at[k], x_dev(x, k + 1)) for k in range(3)]
    for d in sends:
        d.start()
    for j in range(4):

        @pl.when(x == j)
        def _():
            gb[0:1, :] = gain3[n_loc * j : n_loc * j + n_loc].reshape(1, n_loc)
            gb[1:2, :] = bias3[n_loc * j : n_loc * j + n_loc].reshape(1, n_loc)

    idx = column(mi[...].astype(F32))
    toks = lax.broadcasted_iota(jnp.int32, (merged, 1024), 1).astype(F32)
    seg_of = jnp.sum(jnp.where(idx[:, 0:1] == toks, seg[...].astype(F32), 0.0), axis=1, keepdims=True)
    names = lax.broadcasted_iota(jnp.int32, (merged, n_tok), 1).astype(F32)
    owner = jnp.sum(jnp.where(seg_of == names, owners[...].astype(F32), 0.0), axis=1, keepdims=True)
    mine = (owner == names).astype(F32)
    below = lax.broadcasted_iota(jnp.int32, (merged, merged), 1) < lax.broadcasted_iota(
        jnp.int32, (merged, merged), 0
    )
    before = jnp.dot(
        jnp.where(below, 1.0, 0.0).astype(BF), mine.astype(BF), preferred_element_type=F32
    )
    rank = jnp.sum(before * mine, axis=1, keepdims=True)
    target = jnp.broadcast_to(owner * slot + rank, (merged, 128)).T[0:1]
    spots = lax.broadcasted_iota(jnp.int32, (n_tok * slot, merged), 0).astype(F32)
    placed[...] = jnp.where(spots == target, 1.0, 0.0).astype(BF)
    for d in sends:
        d.wait_recv()
    means = [st[s, 0:1, :] for s in range(4)]
    mean = 0.25 * (means[0] + means[1] + means[2] + means[3])
    m2 = st[0, 1:2, :] + st[1, 1:2, :] + st[2, 1:2, :] + st[3, 1:2, :]
    for s in range(4):
        d = means[s] - mean
        m2 = m2 + n_loc * (d * d)
    rstd = lax.rsqrt(m2 * (1.0 / (4 * n_loc)) + EPS)
    for i in range(8):
        sl = slice(128 * i, 128 * i + 128)
        row = lax.broadcasted_iota(jnp.int32, (128, 128), 0)
        cols = jnp.where(row == 0, mean[:, sl], jnp.where(row == 1, rstd[:, sl], 0.0)).T
        v = lo[sl, :].astype(F32)
        fin[sl, :] = ((v - cols[:, 0:1]) * cols[:, 1:2] * gb[0:1, :] + gb[1:2, :]).astype(BF)
    load.wait()
    got = []
    for k in range(4):
        pick = jnp.where(idx[:, k : k + 1] == toks, 1.0, 0.0).astype(BF)
        got.append(jnp.dot(pick, fin[...], preferred_element_type=F32).astype(BF))
    for j in range(4):
        acc = jnp.dot(got[0], wpg[j], preferred_element_type=F32)
        for k in range(1, 4):
            acc += jnp.dot(got[k], wpg[k * 4 + j], preferred_element_type=F32)
        own[j] = acc
        sbuf[j] = acc.astype(BF)
    rg = RingReduce(sbuf, far_in, main_in, lambda k: xs.at[k], lambda k: xr.at[k], 128)
    rg.start()
    rg.relay()
    rg.wait()
    total = own[x] + main_in[0].astype(F32) + main_in[1].astype(F32) + pb[...]
    going = jnp.dot(placed[...], total.astype(BF), preferred_element_type=F32).astype(BF)
    obuf[...] = going.reshape(n_tok, slot, n_loc)

    def slot_copy(i):
        to = (t + i) % n_tok
        return rcopy(obuf.at[to], out.at[t], ts.at[i], tr.at[i], {"tok": to})

    @pl.loop(1, n_tok)
    def _(i):
        slot_copy(i).start()

    keep = pltpu.make_async_copy(obuf.at[t], out.at[t], lsem.at[1])
    keep.start()
    rg.finish()
    for d in sends:
        d.wait_send()
    keep.wait()

    @pl.loop(1, n_tok)
    def _(i):
        slot_copy(i).wait()


def kernel_call(body, name, cid, ins, outs, out_specs, scratch, args):
    return pl.pallas_call(
        body,
        name=name,
        out_shape=outs,
        in_specs=ins,
        out_specs=out_specs,
        scratch_shapes=scratch,
        compiler_params=pltpu.CompilerParams(
            collective_id=cid, has_side_effects=True, vmem_limit_bytes=VLIM
        ),
    )(*args)


def sds(shape, dtype):
    return jax.ShapeDtypeStruct(shape, dtype)


DMA = pltpu.SemaphoreType.DMA


def body(
    tokens,
    segment_ids,
    merge_index,
    segment_owner,
    ln1_gain,
    ln1_bias,
    w_qkv,
    qkv_bias,
    w_out,
    out_bias,
    ln2_gain,
    ln2_bias,
    w_fc1,
    fc1_bias,
    w_fc2,
    fc2_bias,
    ln3_gain,
    ln3_bias,
    w_proj,
    proj_bias,
):
    tok = tokens[0]
    width = tok.shape[1]
    part_w = w_qkv.shape[2]
    depth = w_qkv.shape[1]
    heads = part_w // HD
    cols = 3 * heads * HPAD
    hidden = w_fc1.shape[1]
    perm = []
    for bx in range(4):
        for t in range(32):
            ty, tz, tc = t // 8, (t // 2) % 4, t % 2
            perm.append((bx * 32 + t, tz * 32 + (ty * 4 + bx) * 2 + tc))
    wp = lax.ppermute(w_proj, ("blk", "tok"), perm)
    toks, qkv, wof = kernel_call(
        k_qkv,
        "qkv",
        1,
        [VM] * 6,
        [sds((4, 256, width), BF), sds((3 * heads, 1024, HPAD), BF), sds((4, width, part_w), BF)],
        [ANY] * 3,
        [
            pltpu.VMEM((depth, cols), BF),
            pltpu.VMEM((1, cols), F32),
            pltpu.VMEM((4, depth, part_w), BF),
            pltpu.VMEM((4, 256, width), BF),
            pltpu.VMEM((3 * heads, 1024, HPAD), BF),
            pltpu.VMEM((32, depth, cols), BF),
            pltpu.VMEM((32, 4, depth, part_w), BF),
            pltpu.VMEM((width, cols), BF),
            pltpu.VMEM((4, width, part_w), BF),
            pltpu.VMEM((4, 256, width), BF),
            DMA((3,)),
            DMA((6,)),
            DMA((6,)),
            DMA((6,)),
            DMA((3,)),
            DMA((3,)),
        ]
        + TOK_SEMS * 2,
        (tok, w_qkv, w_out, ln1_gain, ln1_bias, qkv_bias),
    )
    lo, wpg = kernel_call(
        k_layer,
        "layer",
        2,
        [VM, VM, ANY, ANY, VM, VM, VM, ANY, VM, ANY, VM, VM],
        [sds((1024, part_w), BF), sds((32, 208, part_w), BF)],
        [VM, ANY],
        [
            pltpu.VMEM((4, 256, width), BF),
            pltpu.VMEM((4, width, part_w), BF),
            pltpu.VMEM((width, hidden), BF),
            pltpu.VMEM((hidden, width), BF),
            pltpu.VMEM((4, 1024, part_w), BF),
            pltpu.VMEM((heads, 256, HPAD), BF),
            pltpu.VMEM((1024, 128), F32),
            pltpu.VMEM((256, width), F32),
            pltpu.VMEM((256, width), BF),
            pltpu.VMEM((256, hidden), BF),
            pltpu.VMEM((4, 256, part_w), F32),
            pltpu.VMEM((4, 4, 256, part_w), BF),
            pltpu.VMEM((4, 2, 128, part_w), BF),
            pltpu.VMEM((4, 2, 256, part_w), BF),
            DMA((5,)),
            DMA((4, 6)),
            DMA((4, 6)),
            DMA((4, 6)),
            DMA((4, 6)),
        ]
        + TOK_SEMS,
        (
            qkv, segment_ids, toks, wof, out_bias, ln2_gain, ln2_bias,
            w_fc1, fc1_bias, w_fc2, fc2_bias, wp,
        ),
    )
    merged_count = merge_index.shape[1]
    n_tok = lax.axis_size("tok")
    slot = 2 * merged_count // n_tok
    arrived = kernel_call(
        k_merge,
        "merge",
        3,
        [VM] * 6 + [ANY, VM],
        [sds((n_tok, slot, part_w), BF)],
        [VM],
        [
            pltpu.VMEM((16, part_w, part_w), BF),
            pltpu.VMEM((1024, part_w), BF),
            pltpu.VMEM((2, part_w), F32),
            pltpu.VMEM((4, 256, part_w), BF),
            pltpu.VMEM((4, 256, part_w), F32),
            pltpu.VMEM((2, 128, part_w), BF),
            pltpu.VMEM((2, 256, part_w), BF),
            pltpu.VMEM((4, 8, 1024), F32),
            pltpu.VMEM((n_tok * slot, merged_count), BF),
            pltpu.VMEM((n_tok, slot, part_w), BF),
            DMA((2,)),
            DMA((3,)),
            DMA((3,)),
            DMA((6,)),
            DMA((6,)),
            DMA((n_tok,)),
            DMA((n_tok,)),
        ],
        (
            lo,
            ln3_gain,
            ln3_bias,
            merge_index[0].T,
            segment_ids,
            segment_owner,
            wpg.reshape(16, part_w, part_w),
            proj_bias,
        ),
    )[0]
    return arrived[None]


def solution(mesh):
    placed = (
        P("tok", "blk", None),
        P("tok", None),
        P("tok", None, None),
        P("tok", None),
        P(),
        P(),
        P(None, "tok", "blk"),
        P(None, "blk"),
        P("blk", "tok"),
        P(),
        P(),
        P(),
        P(None, "blk"),
        P("blk"),
        P("blk", None),
        P(),
        P(),
        P(),
        P("tok", "blk"),
        P("blk"),
    )
    return jax.shard_map(
        body, mesh=mesh, in_specs=placed, out_specs=P("tok", None, None, "blk"), check_vma=False
    )
```

time: 254 us -> 221 us (0.87)
  blocking collectives: 20.4 us -> 0 us
  local copies, waits for them, and re-layouts: 21.1 us -> 4.13 us
  Pallas kernels: 205 us -> 214 us
  other arithmetic: 2.87 us -> 0 us
    all_to_all x1 -> x0, blocking collectives: 20.4 us -> none  [body(): lax.all_to_all(outgoing, 'tok', split_axis=0, concat_axis=0, tiled=True)]
    reshape x10 -> x0, local copies, waits for them, and re-layouts: 10.9 us -> none  [the longest x5 6.46 us: row(): return v.reshape(1, -1)]
    pallas_call x4 -> x3, Pallas kernels: 205 us -> 214 us  [kernel_call(): pl.pallas_call(body, name=name, out_shape=outs, in_specs=ins, out_specs=o...]
    dynamic_slice x3 -> x0, local copies, waits for them, and re-layouts: 4.05 us -> none  [mine(): return lax.dynamic_slice_in_dim(v, x * part_w, part_w, 0).reshape(1, -1)]
    unnamed x3 -> x4, local copies, waits for them, and re-layouts: 1.47 us -> 4.13 us
  transfers between devices with their start and end apart: 1 -> 1, of which waited for: 0 -> 0; matrix products, arithmetic and copies ran while one was open for 9% -> 1% of each run, Pallas kernels for 43% -> 37%
where the time goes in v2:
time: 221 us; the launch traced here: 220 us
  Pallas kernels  214 us (97%)
  local copies, waits for them, and re-layouts  4.13 us (2%)
    pallas_call x3, Pallas kernels, kernel_call(): pl.pallas_call(body, name=name, out_shape=outs, in_specs=ins, out_specs=o...  214 us
  transfers between devices with their start and end apart: 1, of which 0 were waited for; matrix products, arithmetic and copies ran while one was open for 1% of the time, Pallas kernels for 37%

profile of v2, /device:TPU:1, one launch (start us, length us, event | category | flops | bytes accessed | tf_op | source)
XLA Modules:
  0.0 220.2 jit_solution(14365191254499752770)
XLA Ops:
  0.0 1.6 collective-permute-start
  1.6 1.6 copy.21.wout
  3.2 82.1 %qkv.1 = (bf16[4,256,1664]{2,1,0:T(8,128)(2,1)}, bf16[12,1024,128]{2,1,0:T(8,128)(2,1)}, bf16[4,1664,416]{2,1,0:T(8,128)(2,1)}) custom-call(bf16[256,1664]{1,0:T(8,128)(2,1)} %bitcast.8, bf16[3,52,416]{2,1,0:T(8,128)(2,1)} %wq.1, bf16[416,52]{1,0:T(8,128)(2,1)} %copy.21.wout, f32[1664]{0:T(1024)} %gain.2, f32[1664]{0:T(1024)} %bias.2, f32[3,416]{1,0:T(4,128)} %qbias.1), custom_call_target="tpu_custom_call" | custom-call | tf_op jit(solution)/shard_map/qkv/pallas_call | solution.py:688
  85.3 0.0 collective-permute-done.wp
  85.3 0.0 copy-start
  85.3 0.7 copy-done
  86.0 93.4 %layer.1 = (bf16[1024,416]{1,0:T(8,128)(2,1)}, bf16[32,208,416]{2,1,0:T(8,128)(2,1)}) custom-call(bf16[12,1024,128]{2,1,0:T(8,128)(2,1)} %get-tuple-element.10.qkv, s32[1,1024]{1,0:T(1,128)} %seg.3, bf16[4,256,1664]{2,1,0:T(8,128)(2,1)} %get-tuple-element.11.toks_h, bf16[4,1664,416]{2,1,0:T(8,128)(2,1)} %get-tuple-element.12.wof_h, f32[1664]{0:T(1024)} %ob.1, ...), custom_call_target="tpu_custom_call" | custom-call | tf_op jit(solution)/shard_map/layer/pallas_call | solution.py:688
  179.4 39.0 %merge.1 = bf16[32,16,416]{2,1,0:T(8,128)(2,1)} custom-call(bf16[1024,416]{1,0:T(8,128)(2,1)} %get-tuple-element.13.lo, f32[1664]{0:T(1024)} %gain3.1, f32[1664]{0:T(1024)} %bias3.1, s32[4,256]{1,0:T(4,128)} %bitcast.9, s32[1,1024]{1,0:T(1,128)} %seg.3, s32[1,32]{1,0:T(1,128)} %owners.1, bf16[16,416,416]{2,1,0:T(8,128)(2,1)} %bitcast.6, f32[416]{0:T(512)} %pb.1), custom_call_target="tpu_custom_call" | custom-call | tf_op jit(solution)/shard_map/merge/pallas_call | solution.py:688
  218.4 1.9 copy.23
Async XLA Ops:
  0.0 85.3 %collective-permute-start = (bf16[208,416]{1,0:T(8,128)(2,1)}, bf16[208,416]{1,0:T(8,128)(2,1)S(1)}, u32[]{:S(2)}, u32[]{:S(2)}) collective-permute-start(bf16[208,416]{1,0:T(8,128)(2,1)} %param.38), channel_id=1, source_target_pairs={{0,0},{1,1},{2,32},{3,33},{4,64},{5,65},{6,96},{7,97},{8,8},{9,9},... | collective-permute-start | bytes 519176 | tf_op jit(solution)/shard_map/ppermute | solution.py:742
  85.3 0.7 copy-start

commit v3 on v2

--- a/solution.py
+++ b/solution.py
@@ -169,47 +169,43 @@
         self.second[h][i][1].start()
         self.cross[h][0][i].start()
 
-    def first_near(self):
-        for h in range(2):
-            f = self.first[h]
-            f[0].wait_recv()
-            f[2].start()
-            self._fan(h, 1)
-            f[1].wait_recv()
-            f[3].start()
-            self._fan(h, 2)
-
-    def first_far(self):
-        for h in range(2):
-            self.first[h][2].wait_recv()
-            self.first[h][3].wait_recv()
-            self._fan(h, 3)
-
-    def second_near(self, i):
-        for h in range(2):
-            f = self.second[h][i]
-            f[0].wait_recv()
-            f[2].start()
-            self.cross[h][1][i].start()
-            f[1].wait_recv()
-            f[3].start()
-            self.cross[h][2][i].start()
-
-    def second_far(self, i):
-        for h in range(2):
-            f = self.second[h][i]
-            f[2].wait_recv()
-            f[3].wait_recv()
-            self.cross[h][3][i].start()
+    def first_near(self, h):
+        f = self.first[h]
+        f[0].wait_recv()
+        f[2].start()
+        self._fan(h, 1)
+        f[1].wait_recv()
+        f[3].start()
+        self._fan(h, 2)
+
+    def first_far(self, h):
+        self.first[h][2].wait_recv()
+        self.first[h][3].wait_recv()
+        self._fan(h, 3)
+
+    def second_near(self, h, i):
+        f = self.second[h][i]
+        f[0].wait_recv()
+        f[2].start()
+        self.cross[h][1][i].start()
+        f[1].wait_recv()
+        f[3].start()
+        self.cross[h][2][i].start()
+
+    def second_far(self, h, i):
+        f = self.second[h][i]
+        f[2].wait_recv()
+        f[3].wait_recv()
+        self.cross[h][3][i].start()
+
+    def wait_cross(self, h, k):
+        for d in self.cross[h][k]:
+            d.wait_recv()
 
     def _all(self):
         for h in range(2):
             for row in self.cross[h]:
                 yield from row
-
-    def wait_all(self):
-        for d in self._all():
-            d.wait_recv()
 
     def finish(self):
         for h in range(2):
@@ -236,31 +232,34 @@
         dst[at, :] = (center * lax.rsqrt(spread + EPS) * gain[...] + bias[...]).astype(dst.dtype)
 
 
-def view_cols(r, h, q):
-    return r.at[:, pl.ds(768 * h, 768)] if q is None else r.at[:, pl.ds(768 * h + 384 * q, 384)]
-
-
-def view_lead(r, h, q):
-    return r.at[pl.ds(2 * h, 2)] if q is None else r.at[pl.ds(2 * h + q, 1)]
-
-
-def view_rows(r, h, q):
-    start, size = ((0, 112), (112, 96))[h]
-    if q is None:
-        return r.at[pl.ds(start, size)]
-    first = (64, 48)[h]
-    return r.at[pl.ds(start, first)] if q == 0 else r.at[pl.ds(start + first, size - first)]
+def view_rows(tiles):
+    first = 16 * ((tiles + 1) // 2)
+    halves = ((0, first), (first, 16 * tiles - first))
+
+    def view(r, h, q):
+        start, size = halves[h]
+        if q is None:
+            return r.at[pl.ds(start, size)]
+        lead = 16 * ((size // 16 + 1) // 2)
+        return r.at[pl.ds(start, lead)] if q == 0 else r.at[pl.ds(start + lead, size - lead)]
+
+    return view
 
 
 def k_qkv(
     tok, wq, wout, gain, bias, qbias, toks_o, qkv_o, wof_o,
-    wl, qb, wo4, toks, qkv, slots, wslots, wf, wof, hb, lsem, osem, xs, xr, ws, wr, *gs
+    pack, qb, wo4, toks, qkv, slots, wf, wof, hb, lsem, osem, xs, xr, ws, wr, *gs
 ):
     x, y, z, c = position()
     t = lax.axis_index("tok")
     depth = wq.shape[1]
     heads = wq.shape[2] // HD
+    nq = 3 * heads
+    no = wof.shape[1] // 128
     meet(x_peers() + [x_dev(x, 2)] + tok_peers())
+    wo_send = [rcopy(wout, wo4.at[x], ws.at[k], wr.at[k], x_dev(x, k + 1)) for k in range(3)]
+    for d in wo_send:
+        d.start()
     ring = RingGather(
         lambda i: tok.at[pl.ds(128 * i, 128)],
         lambda s, i: toks.at[s, pl.ds(128 * i, 128)],
@@ -268,65 +267,54 @@
         lambda k: xr.at[k],
     )
     ring.start()
+    local = [pltpu.make_async_copy(tok, toks.at[x], lsem.at[0])]
+    local[0].start()
     zero = jnp.zeros((depth, HPAD - HD), BF)
     for k in range(3):
         for h in range(heads):
-            at = (k * heads + h) * HPAD
-            wl[:, at : at + HPAD] = jnp.concatenate([wq[k, :, h * HD : h * HD + HD], zero], axis=1)
-            qb[:, at : at + HPAD] = jnp.concatenate(
+            n = k * heads + h
+            piece = wq[k, :, h * HD : h * HD + HD]
+            pack[n * depth : n * depth + depth, :] = jnp.concatenate([piece, zero], axis=1)
+            qb[:, n * HPAD : n * HPAD + HPAD] = jnp.concatenate(
                 [qbias[k : k + 1, h * HD : h * HD + HD], jnp.zeros((1, HPAD - HD), F32)], axis=1
             )
-    wo4[x] = wout[...].T
-    gq = TokGather(wl, slots, view_cols, *gs[:6])
-    go = TokGather(wo4, wslots, view_lead, *gs[6:])
-    gq.start()
-    wo_send = [rcopy(wo4.at[x], wo4.at[x], ws.at[k], wr.at[k], x_dev(x, k + 1)) for k in range(3)]
-    for d in wo_send:
-        d.start()
-    local = [
-        pltpu.make_async_copy(tok, toks.at[x], lsem.at[0]),
-        pltpu.make_async_copy(wl, slots.at[t], lsem.at[1]),
-    ]
-    for d in local:
-        d.start()
-    norm_rows(tok, hb.at[x], gain, bias, 256)
-    gq.first_near()
+    wo4[x] = wout[...]
     for d in wo_send:
         d.wait_recv()
-    go.start()
-    local.append(pltpu.make_async_copy(wo4, wslots.at[t], lsem.at[2]))
-    local[2].start()
-    gq.first_far()
-    gq.second_near(0)
-    ring.relay()
-    for i in range(1, 4):
-        gq.second_near(i)
-    go.first_near()
-    go.first_far()
-    ring.wait_near()
-    local[0].wait()
+    wide = jnp.concatenate([wo4[b] for b in range(4)], axis=1)
+    for n in range(no):
+        at = (nq + n) * depth
+        pack[at : at + depth, :] = wide[:, 128 * n : 128 * n + 128]
+    gath = TokGather(pack, slots, view_rows(pack.shape[0] // 16), *gs)
+    gath.start()
+    local.append(pltpu.make_async_copy(pack, slots.at[t], lsem.at[1]))
+    local[1].start()
+    norm_rows(tok, hb.at[x], gain, bias, 256)
     outs = []
 
     def put(src, dst):
         outs.append(pltpu.make_async_copy(src, dst, osem.at[len(outs)]))
         outs[-1].start()
 
-    for o in (0, 1, 3):
-        s = (x + o) % 4
-        put(toks.at[s], toks_o.at[s])
-        if o:
-            norm_rows(toks.at[s], hb.at[s], gain, bias, 256)
-    for i in range(4):
-        gq.second_far(i)
-    for i in range(4):
-        go.second_near(i)
-    local[1].wait()
-    gq.wait_all()
-
-    @pl.loop(0, 8)
-    def _(g):
-        parts = [slots[4 * g + j] for j in range(4)]
-        wf[pl.ds(pl.multiple_of(g * 208, 16), 208), :] = jnp.concatenate(parts, axis=0)
+    def unpack(g, lo, n, dst):
+        for i in range(n):
+            at = (lo + i) * depth
+            parts = [slots[4 * g + j, at : at + depth, :] for j in range(4)]
+            rows = pl.ds(pl.multiple_of(g * 208, 16), 208)
+            dst[rows, 128 * i : 128 * i + 128] = jnp.concatenate(parts, axis=0)
+
+    def unpack_qkv(k):
+        gath.wait_cross(0, k)
+        yy = (y + gath.OFF[k]) % 4
+
+        @pl.loop(0, 2)
+        def _(p):
+            unpack(2 * yy + p, 0, nq, wf)
+
+    def unpack_out(p):
+        @pl.loop(0, 4)
+        def _(yy):
+            unpack(2 * yy + p, nq, no, wof)
 
     def project(s):
         @pl.loop(0, wf.shape[1] // 256)
@@ -338,21 +326,41 @@
             qkv[2 * j, rows, :] = v[:, :128]
             qkv[2 * j + 1, rows, :] = v[:, 128:]
 
+    for h in range(2):
+        gath.first_near(h)
+    ring.relay()
+    for h in range(2):
+        gath.first_far(h)
+    for i in range(3):
+        for h in range(2):
+            gath.second_near(h, i)
+    for d in local:
+        d.wait()
+    unpack_qkv(0)
+    for h in range(2):
+        gath.second_near(h, 3)
+    ring.wait_near()
+    for o in (0, 1, 3):
+        s = (x + o) % 4
+        put(toks.at[s], toks_o.at[s])
+        if o:
+            norm_rows(toks.at[s], hb.at[s], gain, bias, 256)
+    unpack_qkv(1)
+    unpack_qkv(2)
+    for i in range(4):
+        for h in range(2):
+            gath.second_far(h, i)
+    for k in range(3):
+        gath.wait_cross(1, k)
+    unpack_qkv(3)
+
     @pl.loop(0, 3)
     def _(i):
         project((x + i + i // 2) % 4)
 
-    for i in range(4):
-        go.second_far(i)
-    local[2].wait()
-    go.wait_all()
-
-    @pl.loop(0, 8)
-    def _(g):
-        for b in range(4):
-            parts = [wslots[4 * g + j, b] for j in range(4)]
-            wof[b, pl.ds(pl.multiple_of(g * 208, 16), 208), :] = jnp.concatenate(parts, axis=0)
-
+    unpack_out(z // 2)
+    gath.wait_cross(1, 3)
+    unpack_out(1 - z // 2)
     put(wof, wof_o)
     ring.wait_far()
     far = (x + 2) % 4
@@ -363,8 +371,7 @@
     for d in wo_send:
         d.wait_send()
     ring.finish()
-    gq.finish()
-    go.finish()
+    gath.finish()
     for d in outs:
         d.wait()
 
@@ -415,7 +422,7 @@
 
 def k_layer(
     qkv, seg, toks_h, wof_h, ob, gain, bias, fc1, b1, fc2, b2, wp, lo, wpg,
-    toks, wof, w1, w2, att, oh, segc, after, h2, hid, own, sbuf, far_in, main_in,
+    toks, wof, w1, w2, att, oh, attf, segc, after, h2, hid, own, sbuf, far_in, main_in,
     lsem, as_, ar, xs, xr, *gs
 ):
     x, y, z, c = position()
@@ -432,7 +439,7 @@
     segr = seg[...].astype(F32)
     segc[...] = jnp.broadcast_to(segr, (128, segr.shape[1])).T
     meet(x_peers() + tok_peers())
-    gath = TokGather(wp, wpg, view_rows, *gs)
+    gath = TokGather(wp, wpg, view_rows(wp.shape[0] // 16), *gs)
     gath.start()
     scale = 1.0 / math.sqrt(HD)
     heads = qkv.shape[0] // 3
@@ -471,21 +478,19 @@
 
     attend(0)
     gather_ring(0).start()
-    gath.first_near()
-    gath.first_far()
+    for h in range(2):
+        gath.first_near(h)
     attend(1)
+    gather_ring(0).relay()
     gather_ring(1).start()
-    gather_ring(0).relay()
+    for h in range(2):
+        gath.first_far(h)
     attend(2)
+    gather_ring(1).relay()
     gather_ring(2).start()
-    for i in range(4):
-        gath.second_near(i)
-    gather_ring(1).relay()
     attend(3)
+    gather_ring(2).relay()
     gather_ring(3).start()
-    gather_ring(2).relay()
-    for i in range(4):
-        gath.second_far(i)
     tiles = [(n, min(256, 1664 - n)) for n in range(0, 1664, 256)]
     for d in load[:2]:
         d.wait()
@@ -498,25 +503,30 @@
             rg.wait_near()
             rg.wait_far()
             rows = pl.ds(pl.multiple_of(r * 256, 256), 256)
+            attf[...] = jnp.concatenate([att[b, rows, :] for b in range(4)], axis=1)
             for n, w in tiles:
-                acc = toks[r, :, n : n + w].astype(F32) + ob[n : n + w]
-                for b in range(4):
-                    acc += lax.dot_general(
-                        att[b, rows, :],
-                        wof[b, n : n + w, :],
-                        (((1,), (1,)), ((), ())),
-                        preferred_element_type=F32,
-                    )
-                after[:, n : n + w] = acc
+                acc = lax.dot_general(
+                    attf[...], wof[n : n + w, :], (((1,), (1,)), ((), ())), preferred_element_type=F32
+                )
+                after[:, n : n + w] = acc + toks[r, :, n : n + w].astype(F32) + ob[n : n + w]
 
             @pl.when(r == 0)
             def _():
                 gather_ring(3).relay()
                 load[2].wait()
+                for i in range(4):
+                    for h in range(2):
+                        gath.second_near(h, i)
 
             @pl.when(r > 0)
             def _():
                 reduce_ring(r - 1).relay()
+
+            @pl.when(r == 2)
+            def _():
+                for i in range(4):
+                    for h in range(2):
+                        gath.second_far(h, i)
 
             norm_rows(after, h2, gain, bias, 256)
             for j in range(4):
@@ -561,7 +571,9 @@
             gather_ring(q).finish()
 
     load[4].wait()
-    gath.wait_all()
+    for h in range(2):
+        for k in range(4):
+            gath.wait_cross(h, k)
     gath.finish()
 
 
@@ -733,6 +745,8 @@
     depth = w_qkv.shape[1]
     heads = part_w // HD
     cols = 3 * heads * HPAD
+    blocks = (cols + width) // 128
+    packed = 16 * (-(-blocks * depth // 16))
     hidden = w_fc1.shape[1]
     perm = []
     for bx in range(4):
@@ -745,28 +759,27 @@
         "qkv",
         1,
         [VM] * 6,
-        [sds((4, 256, width), BF), sds((3 * heads, 1024, HPAD), BF), sds((4, width, part_w), BF)],
+        [sds((4, 256, width), BF), sds((3 * heads, 1024, HPAD), BF), sds((width, width), BF)],
         [ANY] * 3,
         [
-            pltpu.VMEM((depth, cols), BF),
+            pltpu.VMEM((packed, 128), BF),
             pltpu.VMEM((1, cols), F32),
             pltpu.VMEM((4, depth, part_w), BF),
             pltpu.VMEM((4, 256, width), BF),
             pltpu.VMEM((3 * heads, 1024, HPAD), BF),
-            pltpu.VMEM((32, depth, cols), BF),
-            pltpu.VMEM((32, 4, depth, part_w), BF),
+            pltpu.VMEM((32, packed, 128), BF),
             pltpu.VMEM((width, cols), BF),
-            pltpu.VMEM((4, width, part_w), BF),
+            pltpu.VMEM((width, width), BF),
             pltpu.VMEM((4, 256, width), BF),
-            DMA((3,)),
+            DMA((2,)),
             DMA((6,)),
             DMA((6,)),
             DMA((6,)),
             DMA((3,)),
             DMA((3,)),
         ]
-        + TOK_SEMS * 2,
-        (tok, w_qkv, w_out, ln1_gain, ln1_bias, qkv_bias),
+        + TOK_SEMS,
+        (tok, w_qkv, w_out.T, ln1_gain, ln1_bias, qkv_bias),
     )
     lo, wpg = kernel_call(
         k_layer,
@@ -777,11 +790,12 @@
         [VM, ANY],
         [
             pltpu.VMEM((4, 256, width), BF),
-            pltpu.VMEM((4, width, part_w), BF),
+            pltpu.VMEM((width, width), BF),
             pltpu.VMEM((width, hidden), BF),
             pltpu.VMEM((hidden, width), BF),
             pltpu.VMEM((4, 1024, part_w), BF),
             pltpu.VMEM((heads, 256, HPAD), BF),
+            pltpu.VMEM((256, width), BF),
             pltpu.VMEM((1024, 128), F32),
             pltpu.VMEM((256, width), F32),
             pltpu.VMEM((256, width), BF),

time: 221 us -> 202 us (0.914)
  Pallas kernels: 214 us -> 198 us
    pallas_call x3, Pallas kernels: 214 us -> 198 us  [kernel_call(): pl.pallas_call(body, name=name, out_shape=outs, in_specs=ins, out_specs=o...]
  transfers between devices with their start and end apart: 1 -> 1, of which waited for: 0 -> 0; matrix products, arithmetic and copies ran while one was open for 1% -> 0% of each run, Pallas kernels for 37% -> 34%
where the time goes in v3:
time: 202 us
  Pallas kernels  198 us (98%)
  local copies, waits for them, and re-layouts  2.55 us (1%)
    pallas_call x3, Pallas kernels, kernel_call(): pl.pallas_call(body, name=name, out_shape=outs, in_specs=ins, out_specs=o...  198 us
  transfers between devices with their start and end apart: 1, of which 0 were waited for; matrix products, arithmetic and copies ran while one was open for 0% of the time, Pallas kernels for 34%

profile of v3, /device:TPU:1, one launch (start us, length us, event | category | flops | bytes accessed | tf_op | source)
XLA Modules:
  0.0 202.2 jit_solution(1016108953077274234)
XLA Ops:
  0.0 1.6 collective-permute-start
  1.6 68.9 %qkv.1 = (bf16[4,256,1664]{2,1,0:T(8,128)(2,1)}, bf16[12,1024,128]{2,1,0:T(8,128)(2,1)}, bf16[1664,1664]{1,0:T(8,128)(2,1)}) custom-call(bf16[256,1664]{1,0:T(8,128)(2,1)} %bitcast.9, bf16[3,52,416]{2,1,0:T(8,128)(2,1)} %wq.1, bf16[52,416]{1,0:T(8,128)(2,1)} %bitcast.10, f32[1664]{0:T(1024)} %gain.2, f32[1664]{0:T(1024)} %bias.2, f32[3,416]{1,0:T(4,128)} %qbias.1), custom_call_target="tpu_custom_call" | custom-call | tf_op jit(solution)/shard_map/qkv/pallas_call | solution.py:700
  70.5 0.0 collective-permute-done.wp
  70.5 0.0 copy-start
  70.5 0.7 copy-done
  71.2 90.2 %layer.1 = (bf16[1024,416]{1,0:T(8,128)(2,1)}, bf16[32,208,416]{2,1,0:T(8,128)(2,1)}) custom-call(bf16[12,1024,128]{2,1,0:T(8,128)(2,1)} %get-tuple-element.10.qkv, s32[1,1024]{1,0:T(1,128)} %seg.3, bf16[4,256,1664]{2,1,0:T(8,128)(2,1)} %get-tuple-element.11.toks_h, bf16[1664,1664]{1,0:T(8,128)(2,1)} %get-tuple-element.12.wof_h, f32[1664]{0:T(1024)} %ob.1, ...), custom_call_target="tpu_custom_call" | custom-call | tf_op jit(solution)/shard_map/layer/pallas_call | solution.py:700
  161.3 39.0 %merge.1 = bf16[32,16,416]{2,1,0:T(8,128)(2,1)} custom-call(bf16[1024,416]{1,0:T(8,128)(2,1)} %get-tuple-element.13.lo, f32[1664]{0:T(1024)} %gain3.1, f32[1664]{0:T(1024)} %bias3.1, s32[4,256]{1,0:T(4,128)} %bitcast.11, s32[1,1024]{1,0:T(1,128)} %seg.3, s32[1,32]{1,0:T(1,128)} %owners.1, bf16[16,416,416]{2,1,0:T(8,128)(2,1)} %bitcast.7, f32[416]{0:T(512)} %pb.1), custom_call_target="tpu_custom_call" | custom-call | tf_op jit(solution)/shard_map/merge/pallas_call | solution.py:700
  200.3 1.9 copy.22
Async XLA Ops:
  0.0 70.5 %collective-permute-start = (bf16[208,416]{1,0:T(8,128)(2,1)}, bf16[208,416]{1,0:T(8,128)(2,1)S(1)}, u32[]{:S(2)}, u32[]{:S(2)}) collective-permute-start(bf16[208,416]{1,0:T(8,128)(2,1)} %param.38), channel_id=1, source_target_pairs={{0,0},{1,1},{2,32},{3,33},{4,64},{5,65},{6,96},{7,97},{8,8},{9,9},... | collective-permute-start | bytes 519176 | tf_op jit(solution)/shard_map/ppermute | solution.py:756
  70.5 0.7 copy-start

commit v4 on v3

--- a/solution.py
+++ b/solution.py
@@ -376,6 +376,27 @@
         d.wait()
 
 
+def pack_rows(v, dst):
+    rows, width = v.shape
+    full = width // 128
+    rest = width - 128 * full
+    for i in range(full):
+        dst[rows * i : rows * i + rows] = v[:, 128 * i : 128 * i + 128]
+    n = 128 // rest
+    part = rows // n
+    tail = [v[part * q : part * q + part, 128 * full :] for q in range(n)]
+    dst[rows * full : rows * full + part] = jnp.concatenate(tail, axis=1)
+
+
+def unpack_rows(src, rows=256, rest=32):
+    n = 128 // rest
+    part = rows // n
+    full = (src.shape[0] - part) // rows
+    last = src[rows * full : rows * full + part]
+    tail = jnp.concatenate([last[:, rest * q : rest * q + rest] for q in range(n)], axis=0)
+    return jnp.concatenate([src[rows * i : rows * i + rows] for i in range(full)] + [tail], axis=1)
+
+
 class RingReduce:
     def __init__(self, sbuf, far_in, main_in, ss, rs, half):
         x = lax.axis_index("blk")
@@ -422,7 +443,7 @@
 
 def k_layer(
     qkv, seg, toks_h, wof_h, ob, gain, bias, fc1, b1, fc2, b2, wp, lo, wpg,
-    toks, wof, w1, w2, att, oh, attf, segc, after, h2, hid, own, sbuf, far_in, main_in,
+    toks, wof, w1, w2, att, oh, attf, segc, after, h2, hid, own, mine, sbuf, far_in, main_in,
     lsem, as_, ar, xs, xr, *gs
 ):
     x, y, z, c = position()
@@ -442,6 +463,7 @@
     gath = TokGather(wp, wpg, view_rows(wp.shape[0] // 16), *gs)
     gath.start()
     scale = 1.0 / math.sqrt(HD)
+    half = att.shape[2] // 2
     heads = qkv.shape[0] // 3
 
     def attend(r):
@@ -458,11 +480,11 @@
                 o = jnp.dot(p.astype(BF), qkv[2 * heads + h], preferred_element_type=F32) / total
                 oh[h, pl.ds(pl.multiple_of(sub * 128, 128), 128), :] = o.astype(BF)
 
-        att[x, pl.ds(r * 256, 256), :] = jnp.concatenate([oh[h][:, :HD] for h in range(heads)], axis=1)
+        pack_rows(jnp.concatenate([oh[h][:, :HD] for h in range(heads)], axis=1), att.at[x, r])
 
     def gather_ring(r):
         def part(s, i):
-            return att.at[s, pl.ds(pl.multiple_of(r * 256 + 128 * i, 128), 128)]
+            return att.at[s, r, pl.ds(half * i, half)]
 
         return RingGather(lambda i: part(x, i), part, lambda k: as_.at[r, k], lambda k: ar.at[r, k])
 
@@ -473,7 +495,7 @@
             main_in.at[r],
             lambda k: xs.at[r, k],
             lambda k: xr.at[r, k],
-            128,
+            half,
         )
 
     attend(0)
@@ -502,8 +524,7 @@
             rg = gather_ring(r)
             rg.wait_near()
             rg.wait_far()
-            rows = pl.ds(pl.multiple_of(r * 256, 256), 256)
-            attf[...] = jnp.concatenate([att[b, rows, :] for b in range(4)], axis=1)
+            attf[...] = jnp.concatenate([unpack_rows(att.at[b, r]) for b in range(4)], axis=1)
             for n, w in tiles:
                 acc = lax.dot_general(
                     attf[...], wof[n : n + w, :], (((1,), (1,)), ((), ())), preferred_element_type=F32
@@ -533,7 +554,7 @@
 
                 @pl.when(x == j)
                 def _():
-                    own[r] = after[:, 416 * j : 416 * j + 416] + b2[416 * j : 416 * j + 416]
+                    pack_rows(after[:, 416 * j : 416 * j + 416] + b2[416 * j : 416 * j + 416], own.at[r])
 
             for j in range(8):
                 cols = slice(256 * j, 256 * j + 256)
@@ -548,11 +569,12 @@
                 after[:, n : n + w] = jnp.dot(hid[...], w2[:, n : n + w], preferred_element_type=F32)
             for j in range(4):
                 piece = after[:, 416 * j : 416 * j + 416]
-                sbuf[r, j] = piece.astype(BF)
+                pack_rows(piece.astype(BF), sbuf.at[r, j])
 
                 @pl.when(x == j)
                 def _():
-                    own[r] += piece
+                    pack_rows(piece, mine)
+                    own[r] += mine[...]
 
             reduce_ring(r).start()
 
@@ -566,7 +588,7 @@
             rg = reduce_ring(q)
             rg.wait()
             total = own[q] + main_in[q, 0].astype(F32) + main_in[q, 1].astype(F32)
-            lo[pl.ds(pl.multiple_of(q * 256, 256), 256), :] = total.astype(BF)
+            lo[q] = total.astype(BF)
             rg.finish()
             gather_ring(q).finish()
 
@@ -584,14 +606,14 @@
 
 def k_merge(
     lo, gain3, bias3, mi, seg, owners, wpg_h, pb, out,
-    wpg, fin, gb, sbuf, own, far_in, main_in, st, placed, obuf, lsem, ss, sr, xs, xr, ts, tr
+    wpg, rows_f, fin, gb, sbuf, own, far_in, main_in, st, placed, obuf, lsem, ss, sr, xs, xr, ts, tr
 ):
     x, y, z, c = position()
     t = lax.axis_index("tok")
     n_tok = out.shape[0]
     slot = out.shape[1]
     merged = mi.shape[1]
-    n_loc = lo.shape[1]
+    n_loc = wpg.shape[2]
     load = pltpu.make_async_copy(wpg_h, wpg, lsem.at[0])
     load.start()
     bar = pltpu.get_barrier_semaphore()
@@ -604,14 +626,15 @@
     def _(i):
         pl.semaphore_signal(bar, inc=1, device_id=x_dev(x, i), device_id_type=MESH_ID)
 
-    @pl.loop(0, 8)
+    @pl.loop(0, 4)
     def _(i):
-        rows = pl.ds(pl.multiple_of(i * 128, 128), 128)
-        v = lo[rows, :].astype(F32)
+        rows = pl.ds(pl.multiple_of(i * 256, 256), 256)
+        v = unpack_rows(lo.at[i]).astype(F32)
+        rows_f[rows, :] = v
         mean = jnp.mean(v, axis=-1, keepdims=True)
         d = v - mean
         m2 = jnp.sum(d * d, axis=-1, keepdims=True)
-        lane = lax.broadcasted_iota(jnp.int32, (128, 128), 1)
+        lane = lax.broadcasted_iota(jnp.int32, (256, 128), 1)
         both = jnp.where(lane == 0, mean, jnp.where(lane == 1, m2, 0.0))
         st[x, :, rows] = both.T[:8]
 
@@ -655,7 +678,7 @@
         sl = slice(128 * i, 128 * i + 128)
         row = lax.broadcasted_iota(jnp.int32, (128, 128), 0)
         cols = jnp.where(row == 0, mean[:, sl], jnp.where(row == 1, rstd[:, sl], 0.0)).T
-        v = lo[sl, :].astype(F32)
+        v = rows_f[sl, :]
         fin[sl, :] = ((v - cols[:, 0:1]) * cols[:, 1:2] * gb[0:1, :] + gb[1:2, :]).astype(BF)
     load.wait()
     got = []
@@ -666,13 +689,14 @@
         acc = jnp.dot(got[0], wpg[j], preferred_element_type=F32)
         for k in range(1, 4):
             acc += jnp.dot(got[k], wpg[k * 4 + j], preferred_element_type=F32)
-        own[j] = acc
-        sbuf[j] = acc.astype(BF)
-    rg = RingReduce(sbuf, far_in, main_in, lambda k: xs.at[k], lambda k: xr.at[k], 128)
+        pack_rows(acc, own.at[j])
+        sbuf[j] = own[j].astype(BF)
+    rg = RingReduce(sbuf, far_in, main_in, lambda k: xs.at[k], lambda k: xr.at[k], sbuf.shape[1] // 2)
     rg.start()
     rg.relay()
     rg.wait()
-    total = own[x] + main_in[0].astype(F32) + main_in[1].astype(F32) + pb[...]
+    own[x] += main_in[0].astype(F32) + main_in[1].astype(F32)
+    total = unpack_rows(own.at[x]) + pb[...]
     going = jnp.dot(placed[...], total.astype(BF), preferred_element_type=F32).astype(BF)
     obuf[...] = going.reshape(n_tok, slot, n_loc)
 
@@ -748,6 +772,7 @@
     blocks = (cols + width) // 128
     packed = 16 * (-(-blocks * depth // 16))
     hidden = w_fc1.shape[1]
+    flat = 256 * part_w // 128
     perm = []
     for bx in range(4):
         for t in range(32):
@@ -786,24 +811,25 @@
         "layer",
         2,
         [VM, VM, ANY, ANY, VM, VM, VM, ANY, VM, ANY, VM, VM],
-        [sds((1024, part_w), BF), sds((32, 208, part_w), BF)],
+        [sds((4, flat, 128), BF), sds((32, 208, part_w), BF)],
         [VM, ANY],
         [
             pltpu.VMEM((4, 256, width), BF),
             pltpu.VMEM((width, width), BF),
             pltpu.VMEM((width, hidden), BF),
             pltpu.VMEM((hidden, width), BF),
-            pltpu.VMEM((4, 1024, part_w), BF),
+            pltpu.VMEM((4, 4, flat, 128), BF),
             pltpu.VMEM((heads, 256, HPAD), BF),
             pltpu.VMEM((256, width), BF),
             pltpu.VMEM((1024, 128), F32),
             pltpu.VMEM((256, width), F32),
             pltpu.VMEM((256, width), BF),
             pltpu.VMEM((256, hidden), BF),
-            pltpu.VMEM((4, 256, part_w), F32),
-            pltpu.VMEM((4, 4, 256, part_w), BF),
-            pltpu.VMEM((4, 2, 128, part_w), BF),
-            pltpu.VMEM((4, 2, 256, part_w), BF),
+            pltpu.VMEM((4, flat, 128), F32),
+            pltpu.VMEM((flat, 128), F32),
+            pltpu.VMEM((4, 4, flat, 128), BF),
+            pltpu.VMEM((4, 2, flat // 2, 128), BF),
+            pltpu.VMEM((4, 2, flat, 128), BF),
             DMA((5,)),
             DMA((4, 6)),
             DMA((4, 6)),
@@ -828,12 +854,13 @@
         [VM],
         [
             pltpu.VMEM((16, part_w, part_w), BF),
+            pltpu.VMEM((1024, part_w), F32),
             pltpu.VMEM((1024, part_w), BF),
             pltpu.VMEM((2, part_w), F32),
-            pltpu.VMEM((4, 256, part_w), BF),
-            pltpu.VMEM((4, 256, part_w), F32),
-            pltpu.VMEM((2, 128, part_w), BF),
-            pltpu.VMEM((2, 256, part_w), BF),
+            pltpu.VMEM((4, flat, 128), BF),
+            pltpu.VMEM((4, flat, 128), F32),
+            pltpu.VMEM((2, flat // 2, 128), BF),
+            pltpu.VMEM((2, flat, 128), BF),
             pltpu.VMEM((4, 8, 1024), F32),
             pltpu.VMEM((n_tok * slot, merged_count), BF),
             pltpu.VMEM((n_tok, slot, part_w), BF),

time: 202 us -> 195 us (0.965)
  Pallas kernels: 198 us -> 191 us
    pallas_call x3, Pallas kernels: 198 us -> 191 us  [kernel_call(): pl.pallas_call(body, name=name, out_shape=outs, in_specs=ins, out_specs=o...]
  transfers between devices with their start and end apart: 1 -> 1, of which waited for: 0 -> 0; matrix products, arithmetic and copies ran while one was open for 0% -> 0% of each run, Pallas kernels for 34% -> 35%
where the time goes in v4:
time: 195 us
  Pallas kernels  191 us (98%)
  local copies, waits for them, and re-layouts  2.55 us (1%)
    pallas_call x3, Pallas kernels, kernel_call(): pl.pallas_call(body, name=name, out_shape=outs, in_specs=ins, out_specs=o...  191 us
  transfers between devices with their start and end apart: 1, of which 0 were waited for; matrix products, arithmetic and copies ran while one was open for 0% of the time, Pallas kernels for 35%

profile of v4, /device:TPU:1, one launch (start us, length us, event | category | flops | bytes accessed | tf_op | source)
XLA Modules:
  0.0 194.8 jit_solution(3111095858481748675)
XLA Ops:
  0.0 1.6 collective-permute-start
  1.6 68.9 %qkv.1 = (bf16[4,256,1664]{2,1,0:T(8,128)(2,1)}, bf16[12,1024,128]{2,1,0:T(8,128)(2,1)}, bf16[1664,1664]{1,0:T(8,128)(2,1)}) custom-call(bf16[256,1664]{1,0:T(8,128)(2,1)} %bitcast.9, bf16[3,52,416]{2,1,0:T(8,128)(2,1)} %wq.1, bf16[52,416]{1,0:T(8,128)(2,1)} %bitcast.10, f32[1664]{0:T(1024)} %gain.2, f32[1664]{0:T(1024)} %bias.2, f32[3,416]{1,0:T(4,128)} %qbias.1), custom_call_target="tpu_custom_call" | custom-call | tf_op jit(solution)/shard_map/qkv/pallas_call | solution.py:724
  70.5 0.0 collective-permute-done.wp
  70.5 0.0 copy-start
  70.5 0.7 copy-done
  71.2 84.9 %layer.1 = (bf16[4,832,128]{2,1,0:T(8,128)(2,1)}, bf16[32,208,416]{2,1,0:T(8,128)(2,1)}) custom-call(bf16[12,1024,128]{2,1,0:T(8,128)(2,1)} %get-tuple-element.10.qkv, s32[1,1024]{1,0:T(1,128)} %seg.3, bf16[4,256,1664]{2,1,0:T(8,128)(2,1)} %get-tuple-element.11.toks_h, bf16[1664,1664]{1,0:T(8,128)(2,1)} %get-tuple-element.12.wof_h, f32[1664]{0:T(1024)} %ob.1, ...), custom_call_target="tpu_custom_call" | custom-call | tf_op jit(solution)/shard_map/layer/pallas_call | solution.py:724
  156.1 36.8 %merge.1 = bf16[32,16,416]{2,1,0:T(8,128)(2,1)} custom-call(bf16[4,832,128]{2,1,0:T(8,128)(2,1)} %get-tuple-element.13.lo, f32[1664]{0:T(1024)} %gain3.1, f32[1664]{0:T(1024)} %bias3.1, s32[4,256]{1,0:T(4,128)} %bitcast.11, s32[1,1024]{1,0:T(1,128)} %seg.3, s32[1,32]{1,0:T(1,128)} %owners.1, bf16[16,416,416]{2,1,0:T(8,128)(2,1)} %bitcast.7, f32[416]{0:T(512)} %pb.1), custom_call_target="tpu_custom_call" | custom-call | tf_op jit(solution)/shard_map/merge/pallas_call | solution.py:724
  192.9 1.9 copy.22
Async XLA Ops:
  0.0 70.5 %collective-permute-start = (bf16[208,416]{1,0:T(8,128)(2,1)}, bf16[208,416]{1,0:T(8,128)(2,1)S(1)}, u32[]{:S(2)}, u32[]{:S(2)}) collective-permute-start(bf16[208,416]{1,0:T(8,128)(2,1)} %param.38), channel_id=1, source_target_pairs={{0,0},{1,1},{2,32},{3,33},{4,64},{5,65},{6,96},{7,97},{8,8},{9,9},... | collective-permute-start | bytes 519176 | tf_op jit(solution)/shard_map/ppermute | solution.py:781
  70.5 0.7 copy-start

commit v5 on v4

--- a/solution.py
+++ b/solution.py
@@ -232,6 +232,71 @@
         dst[at, :] = (center * lax.rsqrt(spread + EPS) * gain[...] + bias[...]).astype(dst.dtype)
 
 
+def pack_rows(v, dst):
+    rows, width = v.shape
+    full = width // 128
+    rest = width - 128 * full
+    for i in range(full):
+        dst[rows * i : rows * i + rows] = v[:, 128 * i : 128 * i + 128]
+    n = 128 // rest
+    part = rows // n
+    tail = [v[part * q : part * q + part, 128 * full :] for q in range(n)]
+    dst[rows * full : rows * full + part] = jnp.concatenate(tail, axis=1)
+
+
+def unpack_rows(src, rows=256, rest=32):
+    n = 128 // rest
+    part = rows // n
+    full = (src.shape[0] - part) // rows
+    last = src[rows * full : rows * full + part]
+    tail = jnp.concatenate([last[:, rest * q : rest * q + rest] for q in range(n)], axis=0)
+    return jnp.concatenate([src[rows * i : rows * i + rows] for i in range(full)] + [tail], axis=1)
+
+
+class RingReduce:
+    def __init__(self, sbuf, far_in, main_in, ss, rs, half):
+        x = lax.axis_index("blk")
+        self.hi, self.lo, self.far = (x + 1) % 4, (x + 3) % 4, (x + 2) % 4
+        self.sbuf, self.far_in, self.main_in = sbuf, far_in, main_in
+        right, left = x_dev(x, 1), x_dev(x, 3)
+        self.a, self.b = pl.ds(0, half), pl.ds(half, half)
+        a, b = self.a, self.b
+        self.c = [
+            rcopy(sbuf.at[self.far, a], far_in.at[0], ss(0), rs(0), right),
+            rcopy(sbuf.at[self.far, b], far_in.at[1], ss(1), rs(1), left),
+            rcopy(sbuf.at[self.hi, b], main_in.at[0, b], ss(2), rs(2), right),
+            rcopy(sbuf.at[self.lo, a], main_in.at[1, a], ss(3), rs(3), left),
+            rcopy(sbuf.at[self.hi, a], main_in.at[0, a], ss(4), rs(4), right),
+            rcopy(sbuf.at[self.lo, b], main_in.at[1, b], ss(5), rs(5), left),
+        ]
+
+    def start(self):
+        for k in range(4):
+            self.c[k].start()
+
+    def relay(self):
+        self.c[0].wait_recv()
+        s = self.sbuf[self.hi, self.a].astype(F32) + self.far_in[0].astype(F32)
+        self.sbuf[self.hi, self.a] = s.astype(BF)
+        self.c[1].wait_recv()
+        s = self.sbuf[self.lo, self.b].astype(F32) + self.far_in[1].astype(F32)
+        self.sbuf[self.lo, self.b] = s.astype(BF)
+        self.c[4].start()
+        self.c[5].start()
+
+    def wait(self):
+        for k in range(2, 6):
+            self.c[k].wait_recv()
+
+    def finish(self):
+        for d in self.c:
+            d.wait_send()
+
+
+def gelu(v):
+    return 0.5 * v * (1.0 + lax.erf(v * (1.0 / math.sqrt(2.0))))
+
+
 def view_rows(tiles):
     first = 16 * ((tiles + 1) // 2)
     halves = ((0, first), (first, 16 * tiles - first))
@@ -246,9 +311,10 @@
     return view
 
 
-def k_qkv(
-    tok, wq, wout, gain, bias, qbias, toks_o, qkv_o, wof_o,
-    pack, qb, wo4, toks, qkv, slots, wf, wof, hb, lsem, osem, xs, xr, ws, wr, *gs
+def k_layer(
+    tok, wq, wout, gain1, bias1, qbias, seg, ob, gain2, bias2, fc1, b1, fc2, b2, wp, lo, wpg,
+    pack, qb, wo4, toks, qkv, slots, wf, wof, hb, w1, w2, att, oh, segc, after, hid, own, mine,
+    sbuf, far_in, main_in, lsem, rs, rr, ws, wr, as_, ar, xs, xr, *gs
 ):
     x, y, z, c = position()
     t = lax.axis_index("tok")
@@ -256,6 +322,12 @@
     heads = wq.shape[2] // HD
     nq = 3 * heads
     no = wof.shape[1] // 128
+    h2, attf = hb.at[0], hb.at[1]
+    load = [
+        pltpu.make_async_copy(fc1, w1, lsem.at[2]),
+        pltpu.make_async_copy(fc2, w2, lsem.at[3]),
+        pltpu.make_async_copy(wp, wpg.at[t], lsem.at[4]),
+    ]
     meet(x_peers() + [x_dev(x, 2)] + tok_peers())
     wo_send = [rcopy(wout, wo4.at[x], ws.at[k], wr.at[k], x_dev(x, k + 1)) for k in range(3)]
     for d in wo_send:
@@ -263,8 +335,8 @@
     ring = RingGather(
         lambda i: tok.at[pl.ds(128 * i, 128)],
         lambda s, i: toks.at[s, pl.ds(128 * i, 128)],
-        lambda k: xs.at[k],
-        lambda k: xr.at[k],
+        lambda k: rs.at[k],
+        lambda k: rr.at[k],
     )
     ring.start()
     local = [pltpu.make_async_copy(tok, toks.at[x], lsem.at[0])]
@@ -285,20 +357,19 @@
     for n in range(no):
         at = (nq + n) * depth
         pack[at : at + depth, :] = wide[:, 128 * n : 128 * n + 128]
-    gath = TokGather(pack, slots, view_rows(pack.shape[0] // 16), *gs)
+    gath = TokGather(pack, slots, view_rows(pack.shape[0] // 16), *gs[:6])
     gath.start()
+    for d in load:
+        d.start()
     local.append(pltpu.make_async_copy(pack, slots.at[t], lsem.at[1]))
     local[1].start()
-    norm_rows(tok, hb.at[x], gain, bias, 256)
-    outs = []
-
-    def put(src, dst):
-        outs.append(pltpu.make_async_copy(src, dst, osem.at[len(outs)]))
-        outs[-1].start()
-
-    def unpack(g, lo, n, dst):
+    norm_rows(tok, hb.at[x], gain1, bias1, 256)
+    segr = seg[...].astype(F32)
+    segc[...] = jnp.broadcast_to(segr, (128, segr.shape[1])).T
+
+    def unpack(g, first, n, dst):
         for i in range(n):
-            at = (lo + i) * depth
+            at = (first + i) * depth
             parts = [slots[4 * g + j, at : at + depth, :] for j in range(4)]
             rows = pl.ds(pl.multiple_of(g * 208, 16), 208)
             dst[rows, 128 * i : 128 * i + 128] = jnp.concatenate(parts, axis=0)
@@ -331,140 +402,34 @@
     ring.relay()
     for h in range(2):
         gath.first_far(h)
-    for i in range(3):
+    for i in range(4):
         for h in range(2):
             gath.second_near(h, i)
     for d in local:
         d.wait()
     unpack_qkv(0)
-    for h in range(2):
-        gath.second_near(h, 3)
     ring.wait_near()
-    for o in (0, 1, 3):
+    for o in (1, 3):
         s = (x + o) % 4
-        put(toks.at[s], toks_o.at[s])
-        if o:
-            norm_rows(toks.at[s], hb.at[s], gain, bias, 256)
+        norm_rows(toks.at[s], hb.at[s], gain1, bias1, 256)
     unpack_qkv(1)
     unpack_qkv(2)
     for i in range(4):
-        for h in range(2):
-            gath.second_far(h, i)
-    for k in range(3):
-        gath.wait_cross(1, k)
+        gath.second_far(0, i)
     unpack_qkv(3)
 
     @pl.loop(0, 3)
     def _(i):
         project((x + i + i // 2) % 4)
 
-    unpack_out(z // 2)
-    gath.wait_cross(1, 3)
-    unpack_out(1 - z // 2)
-    put(wof, wof_o)
+    for i in range(4):
+        gath.second_far(1, i)
     ring.wait_far()
     far = (x + 2) % 4
-    put(toks.at[far], toks_o.at[far])
-    norm_rows(toks.at[far], hb.at[far], gain, bias, 256)
+    norm_rows(toks.at[far], hb.at[far], gain1, bias1, 256)
     project(far)
-    put(qkv, qkv_o)
-    for d in wo_send:
-        d.wait_send()
-    ring.finish()
-    gath.finish()
-    for d in outs:
-        d.wait()
-
-
-def pack_rows(v, dst):
-    rows, width = v.shape
-    full = width // 128
-    rest = width - 128 * full
-    for i in range(full):
-        dst[rows * i : rows * i + rows] = v[:, 128 * i : 128 * i + 128]
-    n = 128 // rest
-    part = rows // n
-    tail = [v[part * q : part * q + part, 128 * full :] for q in range(n)]
-    dst[rows * full : rows * full + part] = jnp.concatenate(tail, axis=1)
-
-
-def unpack_rows(src, rows=256, rest=32):
-    n = 128 // rest
-    part = rows // n
-    full = (src.shape[0] - part) // rows
-    last = src[rows * full : rows * full + part]
-    tail = jnp.concatenate([last[:, rest * q : rest * q + rest] for q in range(n)], axis=0)
-    return jnp.concatenate([src[rows * i : rows * i + rows] for i in range(full)] + [tail], axis=1)
-
-
-class RingReduce:
-    def __init__(self, sbuf, far_in, main_in, ss, rs, half):
-        x = lax.axis_index("blk")
-        self.hi, self.lo, self.far = (x + 1) % 4, (x + 3) % 4, (x + 2) % 4
-        self.sbuf, self.far_in, self.main_in = sbuf, far_in, main_in
-        right, left = x_dev(x, 1), x_dev(x, 3)
-        self.a, self.b = pl.ds(0, half), pl.ds(half, half)
-        a, b = self.a, self.b
-        self.c = [
-            rcopy(sbuf.at[self.far, a], far_in.at[0], ss(0), rs(0), right),
-            rcopy(sbuf.at[self.far, b], far_in.at[1], ss(1), rs(1), left),
-            rcopy(sbuf.at[self.hi, b], main_in.at[0, b], ss(2), rs(2), right),
-            rcopy(sbuf.at[self.lo, a], main_in.at[1, a], ss(3), rs(3), left),
-            rcopy(sbuf.at[self.hi, a], main_in.at[0, a], ss(4), rs(4), right),
-            rcopy(sbuf.at[self.lo, b], main_in.at[1, b], ss(5), rs(5), left),
-        ]
-
-    def start(self):
-        for k in range(4):
-            self.c[k].start()
-
-    def relay(self):
-        self.c[0].wait_recv()
-        s = self.sbuf[self.hi, self.a].astype(F32) + self.far_in[0].astype(F32)
-        self.sbuf[self.hi, self.a] = s.astype(BF)
-        self.c[1].wait_recv()
-        s = self.sbuf[self.lo, self.b].astype(F32) + self.far_in[1].astype(F32)
-        self.sbuf[self.lo, self.b] = s.astype(BF)
-        self.c[4].start()
-        self.c[5].start()
-
-    def wait(self):
-        for k in range(2, 6):
-            self.c[k].wait_recv()
-
-    def finish(self):
-        for d in self.c:
-            d.wait_send()
-
-
-def gelu(v):
-    return 0.5 * v * (1.0 + lax.erf(v * (1.0 / math.sqrt(2.0))))
-
-
-def k_layer(
-    qkv, seg, toks_h, wof_h, ob, gain, bias, fc1, b1, fc2, b2, wp, lo, wpg,
-    toks, wof, w1, w2, att, oh, attf, segc, after, h2, hid, own, mine, sbuf, far_in, main_in,
-    lsem, as_, ar, xs, xr, *gs
-):
-    x, y, z, c = position()
-    t = lax.axis_index("tok")
-    load = [
-        pltpu.make_async_copy(wof_h, wof, lsem.at[0]),
-        pltpu.make_async_copy(toks_h, toks, lsem.at[1]),
-        pltpu.make_async_copy(fc1, w1, lsem.at[2]),
-        pltpu.make_async_copy(fc2, w2, lsem.at[3]),
-        pltpu.make_async_copy(wp, wpg.at[t], lsem.at[4]),
-    ]
-    for d in load:
-        d.start()
-    segr = seg[...].astype(F32)
-    segc[...] = jnp.broadcast_to(segr, (128, segr.shape[1])).T
-    meet(x_peers() + tok_peers())
-    gath = TokGather(wp, wpg, view_rows(wp.shape[0] // 16), *gs)
-    gath.start()
     scale = 1.0 / math.sqrt(HD)
     half = att.shape[2] // 2
-    heads = qkv.shape[0] // 3
 
     def attend(r):
         @pl.loop(0, 2)
@@ -500,23 +465,22 @@
 
     attend(0)
     gather_ring(0).start()
-    for h in range(2):
-        gath.first_near(h)
     attend(1)
     gather_ring(0).relay()
     gather_ring(1).start()
-    for h in range(2):
-        gath.first_far(h)
     attend(2)
     gather_ring(1).relay()
     gather_ring(2).start()
     attend(3)
     gather_ring(2).relay()
     gather_ring(3).start()
+    for k in range(4):
+        gath.wait_cross(1, k)
+    for p in range(2):
+        unpack_out(p)
+    merg = TokGather(wp, wpg, view_rows(wp.shape[0] // 16), *gs[6:])
+    merg.start()
     tiles = [(n, min(256, 1664 - n)) for n in range(0, 1664, 256)]
-    for d in load[:2]:
-        d.wait()
-
     @pl.loop(0, 6)
     def _(r):
         @pl.when(r < 4)
@@ -534,22 +498,32 @@
             @pl.when(r == 0)
             def _():
                 gather_ring(3).relay()
-                load[2].wait()
-                for i in range(4):
-                    for h in range(2):
-                        gath.second_near(h, i)
+                load[0].wait()
 
             @pl.when(r > 0)
             def _():
                 reduce_ring(r - 1).relay()
+
+            @pl.when(r == 1)
+            def _():
+                for h in range(2):
+                    merg.first_near(h)
+                for h in range(2):
+                    merg.first_far(h)
 
             @pl.when(r == 2)
             def _():
                 for i in range(4):
                     for h in range(2):
-                        gath.second_far(h, i)
-
-            norm_rows(after, h2, gain, bias, 256)
+                        merg.second_near(h, i)
+
+            @pl.when(r == 3)
+            def _():
+                for i in range(4):
+                    for h in range(2):
+                        merg.second_far(h, i)
+
+            norm_rows(after, h2, gain2, bias2, 256)
             for j in range(4):
 
                 @pl.when(x == j)
@@ -563,7 +537,7 @@
 
             @pl.when(r == 0)
             def _():
-                load[3].wait()
+                load[1].wait()
 
             for n, w in tiles:
                 after[:, n : n + w] = jnp.dot(hid[...], w2[:, n : n + w], preferred_element_type=F32)
@@ -592,11 +566,15 @@
             rg.finish()
             gather_ring(q).finish()
 
-    load[4].wait()
+    load[2].wait()
     for h in range(2):
         for k in range(4):
-            gath.wait_cross(h, k)
+            merg.wait_cross(h, k)
+    for d in wo_send:
+        d.wait_send()
+    ring.finish()
     gath.finish()
+    merg.finish()
 
 
 def column(rows):
@@ -779,13 +757,13 @@
             ty, tz, tc = t // 8, (t // 2) % 4, t % 2
             perm.append((bx * 32 + t, tz * 32 + (ty * 4 + bx) * 2 + tc))
     wp = lax.ppermute(w_proj, ("blk", "tok"), perm)
-    toks, qkv, wof = kernel_call(
-        k_qkv,
-        "qkv",
+    lo, wpg = kernel_call(
+        k_layer,
+        "layer",
         1,
-        [VM] * 6,
-        [sds((4, 256, width), BF), sds((3 * heads, 1024, HPAD), BF), sds((width, width), BF)],
-        [ANY] * 3,
+        [VM] * 10 + [ANY, VM, ANY, VM, VM],
+        [sds((4, flat, 128), BF), sds((32, 208, part_w), BF)],
+        [VM, ANY],
         [
             pltpu.VMEM((packed, 128), BF),
             pltpu.VMEM((1, cols), F32),
@@ -796,34 +774,12 @@
             pltpu.VMEM((width, cols), BF),
             pltpu.VMEM((width, width), BF),
             pltpu.VMEM((4, 256, width), BF),
-            DMA((2,)),
-            DMA((6,)),
-            DMA((6,)),
-            DMA((6,)),
-            DMA((3,)),
-            DMA((3,)),
-        ]
-        + TOK_SEMS,
-        (tok, w_qkv, w_out.T, ln1_gain, ln1_bias, qkv_bias),
-    )
-    lo, wpg = kernel_call(
-        k_layer,
-        "layer",
-        2,
-        [VM, VM, ANY, ANY, VM, VM, VM, ANY, VM, ANY, VM, VM],
-        [sds((4, flat, 128), BF), sds((32, 208, part_w), BF)],
-        [VM, ANY],
-        [
-            pltpu.VMEM((4, 256, width), BF),
-            pltpu.VMEM((width, width), BF),
             pltpu.VMEM((width, hidden), BF),
             pltpu.VMEM((hidden, width), BF),
             pltpu.VMEM((4, 4, flat, 128), BF),
             pltpu.VMEM((heads, 256, HPAD), BF),
-            pltpu.VMEM((256, width), BF),
             pltpu.VMEM((1024, 128), F32),
             pltpu.VMEM((256, width), F32),
-            pltpu.VMEM((256, width), BF),
             pltpu.VMEM((256, hidden), BF),
             pltpu.VMEM((4, flat, 128), F32),
             pltpu.VMEM((flat, 128), F32),
@@ -831,15 +787,19 @@
             pltpu.VMEM((4, 2, flat // 2, 128), BF),
             pltpu.VMEM((4, 2, flat, 128), BF),
             DMA((5,)),
+            DMA((6,)),
+            DMA((6,)),
+            DMA((3,)),
+            DMA((3,)),
             DMA((4, 6)),
             DMA((4, 6)),
             DMA((4, 6)),
             DMA((4, 6)),
         ]
-        + TOK_SEMS,
+        + TOK_SEMS * 2,
         (
-            qkv, segment_ids, toks, wof, out_bias, ln2_gain, ln2_bias,
-            w_fc1, fc1_bias, w_fc2, fc2_bias, wp,
+            tok, w_qkv, w_out.T, ln1_gain, ln1_bias, qkv_bias, segment_ids, out_bias, ln2_gain,
+            ln2_bias, w_fc1, fc1_bias, w_fc2, fc2_bias, wp,
         ),
     )
     merged_count = merge_index.shape[1]

time: 195 us -> 198 us (1.015)
  Pallas kernels: 191 us -> 193 us
    pallas_call x3 -> x2, Pallas kernels: 191 us -> 193 us  [kernel_call(): pl.pallas_call(body, name=name, out_shape=outs, in_specs=ins, out_specs=o...]
  transfers between devices with their start and end apart: 1 -> 1, of which waited for: 0 -> 0; matrix products, arithmetic and copies ran while one was open for 0% -> 0% of each run, Pallas kernels for 35% -> 0%
where the time goes in v5:
time: 198 us; the launch traced here: 197 us
  Pallas kernels  193 us (97%)
  local copies, waits for them, and re-layouts  2.55 us (1%)
    pallas_call x2, Pallas kernels, kernel_call(): pl.pallas_call(body, name=name, out_shape=outs, in_specs=ins, out_specs=o...  193 us
  transfers between devices with their start and end apart: 1, of which 0 were waited for; matrix products, arithmetic and copies ran while one was open for 0% of the time, Pallas kernels for 0%

profile of v5, /device:TPU:1, one launch (start us, length us, event | category | flops | bytes accessed | tf_op | source)
XLA Modules:
  0.0 197.3 jit_solution(3154609286844993619)
XLA Ops:
  0.0 1.6 collective-permute-start
  1.6 0.0 collective-permute-done.wp
  1.6 0.0 copy-start
  1.6 0.7 copy-done
  2.3 161.4 %layer.1 = (bf16[4,832,128]{2,1,0:T(8,128)(2,1)}, bf16[32,208,416]{2,1,0:T(8,128)(2,1)}) custom-call(bf16[256,1664]{1,0:T(8,128)(2,1)} %bitcast.9, bf16[3,52,416]{2,1,0:T(8,128)(2,1)} %wq.1, bf16[52,416]{1,0:T(8,128)(2,1)} %bitcast.10, f32[1664]{0:T(1024)} %gain1.1, f32[1664]{0:T(1024)} %bias1.1, f32[3,416]{1,0:T(4,128)} %qbias.1, s32[1,1024]{1,0:T(1,128)} %seg.3, ...), custom_call_target="tpu_custom_call" | custom-call | tf_op jit(solution)/shard_map/layer/pallas_call | solution.py:702
  163.6 31.8 %merge.1 = bf16[32,16,416]{2,1,0:T(8,128)(2,1)} custom-call(bf16[4,832,128]{2,1,0:T(8,128)(2,1)} %get-tuple-element.7.lo, f32[1664]{0:T(1024)} %gain3.1, f32[1664]{0:T(1024)} %bias3.1, s32[4,256]{1,0:T(4,128)} %bitcast.11, s32[1,1024]{1,0:T(1,128)} %seg.3, s32[1,32]{1,0:T(1,128)} %owners.1, bf16[16,416,416]{2,1,0:T(8,128)(2,1)} %bitcast.7, f32[416]{0:T(512)} %pb.1), custom_call_target="tpu_custom_call" | custom-call | tf_op jit(solution)/shard_map/merge/pallas_call | solution.py:702
  195.4 1.9 copy.22
Async XLA Ops:
  0.0 1.6 collective-permute-start
  1.6 0.7 copy-start

commit v6 on v5

--- a/solution.py
+++ b/solution.py
@@ -313,7 +313,7 @@
 
 def k_layer(
     tok, wq, wout, gain1, bias1, qbias, seg, ob, gain2, bias2, fc1, b1, fc2, b2, wp, lo, wpg,
-    pack, qb, wo4, toks, qkv, slots, wf, wof, hb, w1, w2, att, oh, segc, after, hid, own, mine,
+    pack, packo, vec, qb, wo4, toks, qkv, slots, oslots, wf, wof, hb, w1, w2, att, oh, segc, after, hid, own, mine,
     sbuf, far_in, main_in, lsem, rs, rr, ws, wr, as_, ar, xs, xr, *gs
 ):
     x, y, z, c = position()
@@ -323,6 +323,7 @@
     nq = 3 * heads
     no = wof.shape[1] // 128
     h2, attf = hb.at[0], hb.at[1]
+    width = tok.shape[1]
     load = [
         pltpu.make_async_copy(fc1, w1, lsem.at[2]),
         pltpu.make_async_copy(fc2, w2, lsem.at[3]),
@@ -339,6 +340,10 @@
         lambda k: rr.at[k],
     )
     ring.start()
+    for i, v in enumerate((gain1, bias1, gain2, bias2, ob, b2, b1)):
+        vec[i : i + 1, : v.shape[0]] = v[...].reshape(1, v.shape[0])
+    gain1, bias1, gain2, bias2, ob, b2 = [vec.at[i : i + 1, :width] for i in range(6)]
+    b1 = vec.at[6:7]
     local = [pltpu.make_async_copy(tok, toks.at[x], lsem.at[0])]
     local[0].start()
     zero = jnp.zeros((depth, HPAD - HD), BF)
@@ -350,42 +355,38 @@
             qb[:, n * HPAD : n * HPAD + HPAD] = jnp.concatenate(
                 [qbias[k : k + 1, h * HD : h * HD + HD], jnp.zeros((1, HPAD - HD), F32)], axis=1
             )
+    gath = TokGather(pack, slots, view_rows(pack.shape[0] // 16), *gs[:6])
+    gath.start()
     wo4[x] = wout[...]
     for d in wo_send:
         d.wait_recv()
     wide = jnp.concatenate([wo4[b] for b in range(4)], axis=1)
     for n in range(no):
-        at = (nq + n) * depth
-        pack[at : at + depth, :] = wide[:, 128 * n : 128 * n + 128]
-    gath = TokGather(pack, slots, view_rows(pack.shape[0] // 16), *gs[:6])
-    gath.start()
+        packo[n * depth : n * depth + depth, :] = wide[:, 128 * n : 128 * n + 128]
+    gout = TokGather(packo, oslots, view_rows(packo.shape[0] // 16), *gs[6:12])
+    local.append(pltpu.make_async_copy(pack, slots.at[t], lsem.at[1]))
+    local[1].start()
     for d in load:
         d.start()
-    local.append(pltpu.make_async_copy(pack, slots.at[t], lsem.at[1]))
-    local[1].start()
     norm_rows(tok, hb.at[x], gain1, bias1, 256)
     segr = seg[...].astype(F32)
     segc[...] = jnp.broadcast_to(segr, (128, segr.shape[1])).T
 
-    def unpack(g, first, n, dst):
+    def unpack(g, src, n, dst):
         for i in range(n):
-            at = (first + i) * depth
-            parts = [slots[4 * g + j, at : at + depth, :] for j in range(4)]
+            at = i * depth
+            parts = [src[4 * g + j, at : at + depth, :] for j in range(4)]
             rows = pl.ds(pl.multiple_of(g * 208, 16), 208)
             dst[rows, 128 * i : 128 * i + 128] = jnp.concatenate(parts, axis=0)
 
-    def unpack_qkv(k):
-        gath.wait_cross(0, k)
-        yy = (y + gath.OFF[k]) % 4
-
-        @pl.loop(0, 2)
-        def _(p):
-            unpack(2 * yy + p, 0, nq, wf)
-
-    def unpack_out(p):
-        @pl.loop(0, 4)
-        def _(yy):
-            unpack(2 * yy + p, nq, no, wof)
+    def unpack_all(gat, src, n, dst):
+        for h in range(2):
+            for k in range(4):
+                gat.wait_cross(h, k)
+
+        @pl.loop(0, 8)
+        def _(g):
+            unpack(g, src, n, dst)
 
     def project(s):
         @pl.loop(0, wf.shape[1] // 256)
@@ -399,31 +400,40 @@
 
     for h in range(2):
         gath.first_near(h)
-    ring.relay()
     for h in range(2):
         gath.first_far(h)
+    for i in range(2):
+        for h in range(2):
+            gath.second_near(h, i)
+    ring.relay()
+    for i in range(2, 4):
+        for h in range(2):
+            gath.second_near(h, i)
+    gout.start()
+    local.append(pltpu.make_async_copy(packo, oslots.at[t], lsem.at[5]))
+    local[2].start()
     for i in range(4):
         for h in range(2):
-            gath.second_near(h, i)
+            gath.second_far(h, i)
     for d in local:
         d.wait()
-    unpack_qkv(0)
     ring.wait_near()
     for o in (1, 3):
         s = (x + o) % 4
         norm_rows(toks.at[s], hb.at[s], gain1, bias1, 256)
-    unpack_qkv(1)
-    unpack_qkv(2)
-    for i in range(4):
-        gath.second_far(0, i)
-    unpack_qkv(3)
+    for h in range(2):
+        gout.first_near(h)
+    unpack_all(gath, slots, nq, wf)
+    for h in range(2):
+        gout.first_far(h)
 
     @pl.loop(0, 3)
     def _(i):
         project((x + i + i // 2) % 4)
 
     for i in range(4):
-        gath.second_far(1, i)
+        for h in range(2):
+            gout.second_near(h, i)
     ring.wait_far()
     far = (x + 2) % 4
     norm_rows(toks.at[far], hb.at[far], gain1, bias1, 256)
@@ -465,6 +475,9 @@
 
     attend(0)
     gather_ring(0).start()
+    for i in range(4):
+        for h in range(2):
+            gout.second_far(h, i)
     attend(1)
     gather_ring(0).relay()
     gather_ring(1).start()
@@ -474,11 +487,8 @@
     attend(3)
     gather_ring(2).relay()
     gather_ring(3).start()
-    for k in range(4):
-        gath.wait_cross(1, k)
-    for p in range(2):
-        unpack_out(p)
-    merg = TokGather(wp, wpg, view_rows(wp.shape[0] // 16), *gs[6:])
+    unpack_all(gout, oslots, no, wof)
+    merg = TokGather(wp, wpg, view_rows(wp.shape[0] // 16), *gs[12:])
     merg.start()
     tiles = [(n, min(256, 1664 - n)) for n in range(0, 1664, 256)]
     @pl.loop(0, 6)
@@ -493,7 +503,7 @@
                 acc = lax.dot_general(
                     attf[...], wof[n : n + w, :], (((1,), (1,)), ((), ())), preferred_element_type=F32
                 )
-                after[:, n : n + w] = acc + toks[r, :, n : n + w].astype(F32) + ob[n : n + w]
+                after[:, n : n + w] = acc + toks[r, :, n : n + w].astype(F32) + ob[:, n : n + w]
 
             @pl.when(r == 0)
             def _():
@@ -528,11 +538,11 @@
 
                 @pl.when(x == j)
                 def _():
-                    pack_rows(after[:, 416 * j : 416 * j + 416] + b2[416 * j : 416 * j + 416], own.at[r])
+                    pack_rows(after[:, 416 * j : 416 * j + 416] + b2[:, 416 * j : 416 * j + 416], own.at[r])
 
             for j in range(8):
                 cols = slice(256 * j, 256 * j + 256)
-                v = jnp.dot(h2[...], w1[:, cols], preferred_element_type=F32) + b1[cols]
+                v = jnp.dot(h2[...], w1[:, cols], preferred_element_type=F32) + b1[:, cols]
                 hid[:, cols] = gelu(v).astype(BF)
 
             @pl.when(r == 0)
@@ -574,6 +584,7 @@
         d.wait_send()
     ring.finish()
     gath.finish()
+    gout.finish()
     merg.finish()
 
 
@@ -747,8 +758,10 @@
     depth = w_qkv.shape[1]
     heads = part_w // HD
     cols = 3 * heads * HPAD
-    blocks = (cols + width) // 128
-    packed = 16 * (-(-blocks * depth // 16))
+
+    def tall(n):
+        return 16 * (-(-(n // 128) * depth // 16))
+
     hidden = w_fc1.shape[1]
     flat = 256 * part_w // 128
     perm = []
@@ -765,12 +778,15 @@
         [sds((4, flat, 128), BF), sds((32, 208, part_w), BF)],
         [VM, ANY],
         [
-            pltpu.VMEM((packed, 128), BF),
+            pltpu.VMEM((tall(cols), 128), BF),
+            pltpu.VMEM((tall(width), 128), BF),
+            pltpu.VMEM((8, hidden), F32),
             pltpu.VMEM((1, cols), F32),
             pltpu.VMEM((4, depth, part_w), BF),
             pltpu.VMEM((4, 256, width), BF),
             pltpu.VMEM((3 * heads, 1024, HPAD), BF),
-            pltpu.VMEM((32, packed, 128), BF),
+            pltpu.VMEM((32, tall(cols), 128), BF),
+            pltpu.VMEM((32, tall(width), 128), BF),
             pltpu.VMEM((width, cols), BF),
             pltpu.VMEM((width, width), BF),
             pltpu.VMEM((4, 256, width), BF),
@@ -786,7 +802,7 @@
             pltpu.VMEM((4, 4, flat, 128), BF),
             pltpu.VMEM((4, 2, flat // 2, 128), BF),
             pltpu.VMEM((4, 2, flat, 128), BF),
-            DMA((5,)),
+            DMA((6,)),
             DMA((6,)),
             DMA((6,)),
             DMA((3,)),
@@ -796,7 +812,7 @@
             DMA((4, 6)),
             DMA((4, 6)),
         ]
-        + TOK_SEMS * 2,
+        + TOK_SEMS * 3,
         (
             tok, w_qkv, w_out.T, ln1_gain, ln1_bias, qkv_bias, segment_ids, out_bias, ln2_gain,
             ln2_bias, w_fc1, fc1_bias, w_fc2, fc2_bias, wp,

time: 198 us -> 196 us (0.990)
  Pallas kernels: 193 us -> 191 us
where the time goes in v6:
time: 196 us; the launch traced here: 195 us
  Pallas kernels  191 us (97%)
  local copies, waits for them, and re-layouts  2.55 us (1%)
    pallas_call x2, Pallas kernels, kernel_call(): pl.pallas_call(body, name=name, out_shape=outs, in_specs=ins, out_specs=o...  191 us
  transfers between devices with their start and end apart: 1, of which 0 were waited for; matrix products, arithmetic and copies ran while one was open for 0% of the time, Pallas kernels for 0%

profile of v6, /device:TPU:1, one launch (start us, length us, event | category | flops | bytes accessed | tf_op | source)
XLA Modules:
  0.0 195.4 jit_solution(13948344450987354917)
XLA Ops:
  0.0 1.6 collective-permute-start
  1.6 0.0 collective-permute-done.wp
  1.6 0.0 copy-start
  1.6 0.7 copy-done
  2.3 150.4 %layer.1 = (bf16[4,832,128]{2,1,0:T(8,128)(2,1)}, bf16[32,208,416]{2,1,0:T(8,128)(2,1)}) custom-call(bf16[256,1664]{1,0:T(8,128)(2,1)} %bitcast.9, bf16[3,52,416]{2,1,0:T(8,128)(2,1)} %wq.1, bf16[52,416]{1,0:T(8,128)(2,1)} %bitcast.10, f32[1664]{0:T(1024)} %gain1.1, f32[1664]{0:T(1024)} %bias1.1, f32[3,416]{1,0:T(4,128)} %qbias.1, s32[1,1024]{1,0:T(1,128)} %seg.3, ...), custom_call_target="tpu_custom_call" | custom-call | tf_op jit(solution)/shard_map/layer/pallas_call | solution.py:713
  152.7 40.8 %merge.1 = bf16[32,16,416]{2,1,0:T(8,128)(2,1)} custom-call(bf16[4,832,128]{2,1,0:T(8,128)(2,1)} %get-tuple-element.7.lo, f32[1664]{0:T(1024)} %gain3.1, f32[1664]{0:T(1024)} %bias3.1, s32[4,256]{1,0:T(4,128)} %bitcast.11, s32[1,1024]{1,0:T(1,128)} %seg.3, s32[1,32]{1,0:T(1,128)} %owners.1, bf16[16,416,416]{2,1,0:T(8,128)(2,1)} %bitcast.7, f32[416]{0:T(512)} %pb.1), custom_call_target="tpu_custom_call" | custom-call | tf_op jit(solution)/shard_map/merge/pallas_call | solution.py:713
  193.5 1.9 copy.22
Async XLA Ops:
  0.0 1.6 collective-permute-start
  1.6 0.7 copy-start

commit v7 on v6

--- a/solution.py
+++ b/solution.py
@@ -221,10 +221,10 @@
 TOK_SEMS = [pltpu.SemaphoreType.DMA((2, 4))] * 2 + [pltpu.SemaphoreType.DMA((2, 4, 4))] * 4
 
 
-def norm_rows(src, dst, gain, bias, rows, step=32):
+def norm_rows(src, dst, gain, bias, rows, first=0, step=32):
     @pl.loop(0, rows // step)
     def _(i):
-        at = pl.ds(pl.multiple_of(i * step, step), step)
+        at = pl.ds(pl.multiple_of(first + i * step, step), step)
         v = src[at, :].astype(F32)
         mean = jnp.mean(v, axis=-1, keepdims=True)
         center = v - mean
@@ -412,15 +412,17 @@
     gout.start()
     local.append(pltpu.make_async_copy(packo, oslots.at[t], lsem.at[5]))
     local[2].start()
-    for i in range(4):
-        for h in range(2):
-            gath.second_far(h, i)
+    lo_x, hi_x = (x + 3) % 4, (x + 1) % 4
+    norm_rows(toks.at[lo_x], hb.at[lo_x], gain1, bias1, 128)
+    norm_rows(toks.at[hi_x], hb.at[hi_x], gain1, bias1, 128, first=128)
     for d in local:
         d.wait()
     ring.wait_near()
-    for o in (1, 3):
-        s = (x + o) % 4
-        norm_rows(toks.at[s], hb.at[s], gain1, bias1, 256)
+    norm_rows(toks.at[lo_x], hb.at[lo_x], gain1, bias1, 128, first=128)
+    norm_rows(toks.at[hi_x], hb.at[hi_x], gain1, bias1, 128)
+    for i in range(4):
+        for h in range(2):
+            gath.second_far(h, i)
     for h in range(2):
         gout.first_near(h)
     unpack_all(gath, slots, nq, wf)
@@ -434,6 +436,8 @@
     for i in range(4):
         for h in range(2):
             gout.second_near(h, i)
+    merg = TokGather(wp, wpg, view_rows(wp.shape[0] // 16), *gs[12:])
+    merg.start()
     ring.wait_far()
     far = (x + 2) % 4
     norm_rows(toks.at[far], hb.at[far], gain1, bias1, 256)
@@ -481,15 +485,17 @@
     attend(1)
     gather_ring(0).relay()
     gather_ring(1).start()
+    for h in range(2):
+        merg.first_near(h)
     attend(2)
     gather_ring(1).relay()
     gather_ring(2).start()
+    for h in range(2):
+        merg.first_far(h)
     attend(3)
     gather_ring(2).relay()
     gather_ring(3).start()
     unpack_all(gout, oslots, no, wof)
-    merg = TokGather(wp, wpg, view_rows(wp.shape[0] // 16), *gs[12:])
-    merg.start()
     tiles = [(n, min(256, 1664 - n)) for n in range(0, 1664, 256)]
     @pl.loop(0, 6)
     def _(r):
@@ -515,13 +521,6 @@
                 reduce_ring(r - 1).relay()
 
             @pl.when(r == 1)
-            def _():
-                for h in range(2):
-                    merg.first_near(h)
-                for h in range(2):
-                    merg.first_far(h)
-
-            @pl.when(r == 2)
             def _():
                 for i in range(4):
                     for h in range(2):

time: 196 us -> 187 us (0.954)
  Pallas kernels: 191 us -> 183 us
    pallas_call x2, Pallas kernels: 191 us -> 183 us  [kernel_call(): pl.pallas_call(body, name=name, out_shape=outs, in_specs=ins, out_specs=o...]
where the time goes in v7:
time: 187 us
  Pallas kernels  183 us (98%)
  local copies, waits for them, and re-layouts  2.55 us (1%)
    pallas_call x2, Pallas kernels, kernel_call(): pl.pallas_call(body, name=name, out_shape=outs, in_specs=ins, out_specs=o...  183 us
  transfers between devices with their start and end apart: 1, of which 0 were waited for; matrix products, arithmetic and copies ran while one was open for 0% of the time, Pallas kernels for 0%

profile of v7, /device:TPU:1, one launch (start us, length us, event | category | flops | bytes accessed | tf_op | source)
XLA Modules:
  0.0 187.2 jit_solution(5507605427212157055)
XLA Ops:
  0.0 1.6 collective-permute-start
  1.6 0.0 collective-permute-done.wp
  1.6 0.0 copy-start
  1.6 0.7 copy-done
  2.3 145.2 %layer.1 = (bf16[4,832,128]{2,1,0:T(8,128)(2,1)}, bf16[32,208,416]{2,1,0:T(8,128)(2,1)}) custom-call(bf16[256,1664]{1,0:T(8,128)(2,1)} %bitcast.9, bf16[3,52,416]{2,1,0:T(8,128)(2,1)} %wq.1, bf16[52,416]{1,0:T(8,128)(2,1)} %bitcast.10, f32[1664]{0:T(1024)} %gain1.1, f32[1664]{0:T(1024)} %bias1.1, f32[3,416]{1,0:T(4,128)} %qbias.1, s32[1,1024]{1,0:T(1,128)} %seg.3, ...), custom_call_target="tpu_custom_call" | custom-call | tf_op jit(solution)/shard_map/layer/pallas_call | solution.py:712
  147.5 37.8 %merge.1 = bf16[32,16,416]{2,1,0:T(8,128)(2,1)} custom-call(bf16[4,832,128]{2,1,0:T(8,128)(2,1)} %get-tuple-element.7.lo, f32[1664]{0:T(1024)} %gain3.1, f32[1664]{0:T(1024)} %bias3.1, s32[4,256]{1,0:T(4,128)} %bitcast.11, s32[1,1024]{1,0:T(1,128)} %seg.3, s32[1,32]{1,0:T(1,128)} %owners.1, bf16[16,416,416]{2,1,0:T(8,128)(2,1)} %bitcast.7, f32[416]{0:T(512)} %pb.1), custom_call_target="tpu_custom_call" | custom-call | tf_op jit(solution)/shard_map/merge/pallas_call | solution.py:712
  185.3 1.9 copy.22
Async XLA Ops:
  0.0 1.6 collective-permute-start
  1.6 0.7 copy-start

commit v8 on v7

--- a/solution.py
+++ b/solution.py
@@ -13,7 +13,7 @@
 BF = jnp.bfloat16
 F32 = jnp.float32
 MESH_ID = pl.DeviceIdType.MESH
-VLIM = 65000 * 1024
+VLIM = 64600 * 1024
 VM = pl.BlockSpec(memory_space=pltpu.VMEM)
 ANY = pl.BlockSpec(memory_space=pl.ANY)
 
@@ -221,7 +221,7 @@
 TOK_SEMS = [pltpu.SemaphoreType.DMA((2, 4))] * 2 + [pltpu.SemaphoreType.DMA((2, 4, 4))] * 4
 
 
-def norm_rows(src, dst, gain, bias, rows, first=0, step=32):
+def norm_rows(src, dst, gain, bias, rows, first=0, step=64):
     @pl.loop(0, rows // step)
     def _(i):
         at = pl.ds(pl.multiple_of(first + i * step, step), step)
@@ -313,7 +313,7 @@
 
 def k_layer(
     tok, wq, wout, gain1, bias1, qbias, seg, ob, gain2, bias2, fc1, b1, fc2, b2, wp, lo, wpg,
-    pack, packo, vec, qb, wo4, toks, qkv, slots, oslots, wf, wof, hb, w1, w2, att, oh, segc, after, hid, own, mine,
+    pack, packo, vec, qb, wo4, toks, qkv, slots, oslots, wps, wof, hb, w1, w2, att, oh, segc, after, hid, own,
     sbuf, far_in, main_in, lsem, rs, rr, ws, wr, as_, ar, xs, xr, *gs
 ):
     x, y, z, c = position()
@@ -323,11 +323,13 @@
     nq = 3 * heads
     no = wof.shape[1] // 128
     h2, attf = hb.at[0], hb.at[1]
+    mine = segc.at[pl.ds(0, own.shape[1])]
+    wf = wof.at[:, pl.ds(0, nq * HPAD)]
     width = tok.shape[1]
     load = [
         pltpu.make_async_copy(fc1, w1, lsem.at[2]),
         pltpu.make_async_copy(fc2, w2, lsem.at[3]),
-        pltpu.make_async_copy(wp, wpg.at[t], lsem.at[4]),
+        pltpu.make_async_copy(wp, wps.at[t], lsem.at[4]),
     ]
     meet(x_peers() + [x_dev(x, 2)] + tok_peers())
     wo_send = [rcopy(wout, wo4.at[x], ws.at[k], wr.at[k], x_dev(x, k + 1)) for k in range(3)]
@@ -436,7 +438,7 @@
     for i in range(4):
         for h in range(2):
             gout.second_near(h, i)
-    merg = TokGather(wp, wpg, view_rows(wp.shape[0] // 16), *gs[12:])
+    merg = TokGather(wp, wps, view_rows(wp.shape[0] // 16), *gs[12:])
     merg.start()
     ring.wait_far()
     far = (x + 2) % 4
@@ -496,6 +498,7 @@
     gather_ring(2).relay()
     gather_ring(3).start()
     unpack_all(gout, oslots, no, wof)
+    save = pltpu.make_async_copy(wps, wpg, lsem.at[0])
     tiles = [(n, min(256, 1664 - n)) for n in range(0, 1664, 256)]
     @pl.loop(0, 6)
     def _(r):
@@ -564,6 +567,11 @@
         @pl.when(r == 4)
         def _():
             reduce_ring(3).relay()
+            load[2].wait()
+            for h in range(2):
+                for k in range(4):
+                    merg.wait_cross(h, k)
+            save.start()
 
         @pl.when(r > 1)
         def _():
@@ -575,10 +583,7 @@
             rg.finish()
             gather_ring(q).finish()
 
-    load[2].wait()
-    for h in range(2):
-        for k in range(4):
-            merg.wait_cross(h, k)
+    save.wait()
     for d in wo_send:
         d.wait_send()
     ring.finish()
@@ -786,7 +791,7 @@
             pltpu.VMEM((3 * heads, 1024, HPAD), BF),
             pltpu.VMEM((32, tall(cols), 128), BF),
             pltpu.VMEM((32, tall(width), 128), BF),
-            pltpu.VMEM((width, cols), BF),
+            pltpu.VMEM((32, 208, part_w), BF),
             pltpu.VMEM((width, width), BF),
             pltpu.VMEM((4, 256, width), BF),
             pltpu.VMEM((width, hidden), BF),
@@ -797,7 +802,6 @@
             pltpu.VMEM((256, width), F32),
             pltpu.VMEM((256, hidden), BF),
             pltpu.VMEM((4, flat, 128), F32),
-            pltpu.VMEM((flat, 128), F32),
             pltpu.VMEM((4, 4, flat, 128), BF),
             pltpu.VMEM((4, 2, flat // 2, 128), BF),
             pltpu.VMEM((4, 2, flat, 128), BF),

time: 187 us -> 183 us (0.979)
  Pallas kernels: 183 us -> 178 us
    pallas_call x2, Pallas kernels: 183 us -> 178 us  [kernel_call(): pl.pallas_call(body, name=name, out_shape=outs, in_specs=ins, out_specs=o...]
where the time goes in v8:
time: 183 us
  Pallas kernels  178 us (97%)
  local copies, waits for them, and re-layouts  2.55 us (1%)
    pallas_call x2, Pallas kernels, kernel_call(): pl.pallas_call(body, name=name, out_shape=outs, in_specs=ins, out_specs=o...  178 us
  transfers between devices with their start and end apart: 1, of which 0 were waited for; matrix products, arithmetic and copies ran while one was open for 0% of the time, Pallas kernels for 0%

profile of v8, /device:TPU:1, one launch (start us, length us, event | category | flops | bytes accessed | tf_op | source)
XLA Modules:
  0.0 182.6 jit_solution(14384383462728721796)
XLA Ops:
  0.0 1.6 collective-permute-start
  1.6 0.0 collective-permute-done.wp
  1.6 0.0 copy-start
  1.6 0.7 copy-done
  2.3 141.5 %layer.1 = (bf16[4,832,128]{2,1,0:T(8,128)(2,1)}, bf16[32,208,416]{2,1,0:T(8,128)(2,1)}) custom-call(bf16[256,1664]{1,0:T(8,128)(2,1)} %bitcast.9, bf16[3,52,416]{2,1,0:T(8,128)(2,1)} %wq.1, bf16[52,416]{1,0:T(8,128)(2,1)} %bitcast.10, f32[1664]{0:T(1024)} %gain1.1, f32[1664]{0:T(1024)} %bias1.1, f32[3,416]{1,0:T(4,128)} %qbias.1, s32[1,1024]{1,0:T(1,128)} %seg.3, ...), custom_call_target="tpu_custom_call" | custom-call | tf_op jit(solution)/shard_map/layer/pallas_call | solution.py:717
  143.8 36.9 %merge.1 = bf16[32,16,416]{2,1,0:T(8,128)(2,1)} custom-call(bf16[4,832,128]{2,1,0:T(8,128)(2,1)} %get-tuple-element.7.lo, f32[1664]{0:T(1024)} %gain3.1, f32[1664]{0:T(1024)} %bias3.1, s32[4,256]{1,0:T(4,128)} %bitcast.11, s32[1,1024]{1,0:T(1,128)} %seg.3, s32[1,32]{1,0:T(1,128)} %owners.1, bf16[16,416,416]{2,1,0:T(8,128)(2,1)} %bitcast.7, f32[416]{0:T(512)} %pb.1), custom_call_target="tpu_custom_call" | custom-call | tf_op jit(solution)/shard_map/merge/pallas_call | solution.py:717
  180.7 1.9 %copy.22 = bf16[1,32,16,416]{3,2,1,0:T(8,128)(2,1)} copy(bf16[1,32,16,416]{3,2,1,0:T(8,128)(2,1)} %bitcast.8) | data formatting | bytes 851968
Async XLA Ops:
  0.0 1.6 collective-permute-start
  1.6 0.7 copy-start

commit v9 on v8

--- a/solution.py
+++ b/solution.py
@@ -390,15 +390,16 @@
         def _(g):
             unpack(g, src, n, dst)
 
-    def project(s):
+    def project(sources):
         @pl.loop(0, wf.shape[1] // 256)
         def _(j):
             cols = pl.ds(pl.multiple_of(j * 256, 256), 256)
-            v = jnp.dot(hb[s], wf[:, cols], preferred_element_type=F32) + qb[:, cols]
-            v = v.astype(BF)
-            rows = pl.ds(pl.multiple_of(s * 256, 256), 256)
-            qkv[2 * j, rows, :] = v[:, :128]
-            qkv[2 * j + 1, rows, :] = v[:, 128:]
+            for s in sources:
+                v = jnp.dot(hb[s], wf[:, cols], preferred_element_type=F32) + qb[:, cols]
+                v = v.astype(BF)
+                rows = pl.ds(pl.multiple_of(s * 256, 256), 256)
+                qkv[2 * j, rows, :] = v[:, :128]
+                qkv[2 * j + 1, rows, :] = v[:, 128:]
 
     for h in range(2):
         gath.first_near(h)
@@ -431,9 +432,7 @@
     for h in range(2):
         gout.first_far(h)
 
-    @pl.loop(0, 3)
-    def _(i):
-        project((x + i + i // 2) % 4)
+    project([x, hi_x, lo_x])
 
     for i in range(4):
         for h in range(2):
@@ -443,7 +442,7 @@
     ring.wait_far()
     far = (x + 2) % 4
     norm_rows(toks.at[far], hb.at[far], gain1, bias1, 256)
-    project(far)
+    project([far])
     scale = 1.0 / math.sqrt(HD)
     half = att.shape[2] // 2
 
@@ -498,6 +497,9 @@
     gather_ring(2).relay()
     gather_ring(3).start()
     unpack_all(gout, oslots, no, wof)
+    for i in range(4):
+        for h in range(2):
+            merg.second_near(h, i)
     save = pltpu.make_async_copy(wps, wpg, lsem.at[0])
     tiles = [(n, min(256, 1664 - n)) for n in range(0, 1664, 256)]
     @pl.loop(0, 6)
@@ -523,13 +525,7 @@
             def _():
                 reduce_ring(r - 1).relay()
 
-            @pl.when(r == 1)
-            def _():
-                for i in range(4):
-                    for h in range(2):
-                        merg.second_near(h, i)
-
-            @pl.when(r == 3)
+            @pl.when(r == 2)
             def _():
                 for i in range(4):
                     for h in range(2):

time: 183 us -> 180 us (0.984)
  Pallas kernels: 178 us -> 176 us
    pallas_call x2, Pallas kernels: 178 us -> 176 us  [kernel_call(): pl.pallas_call(body, name=name, out_shape=outs, in_specs=ins, out_specs=o...]
where the time goes in v9:
time: 180 us
  Pallas kernels  176 us (98%)
  local copies, waits for them, and re-layouts  2.55 us (1%)
    pallas_call x2, Pallas kernels, kernel_call(): pl.pallas_call(body, name=name, out_shape=outs, in_specs=ins, out_specs=o...  176 us
  transfers between devices with their start and end apart: 1, of which 0 were waited for; matrix products, arithmetic and copies ran while one was open for 0% of the time, Pallas kernels for 0%

profile of v9, /device:TPU:1, one launch (start us, length us, event | category | flops | bytes accessed | tf_op | source)
XLA Modules:
  0.0 180.1 jit_solution(1782209691581199153)
XLA Ops:
  0.0 1.6 collective-permute-start
  1.6 0.0 collective-permute-done.wp
  1.6 0.0 copy-start
  1.6 0.7 copy-done
  2.3 139.3 %layer.1 = (bf16[4,832,128]{2,1,0:T(8,128)(2,1)}, bf16[32,208,416]{2,1,0:T(8,128)(2,1)}) custom-call(bf16[256,1664]{1,0:T(8,128)(2,1)} %bitcast.9, bf16[3,52,416]{2,1,0:T(8,128)(2,1)} %wq.1, bf16[52,416]{1,0:T(8,128)(2,1)} %bitcast.10, f32[1664]{0:T(1024)} %gain1.1, f32[1664]{0:T(1024)} %bias1.1, f32[3,416]{1,0:T(4,128)} %qbias.1, s32[1,1024]{1,0:T(1,128)} %seg.3, ...), custom_call_target="tpu_custom_call" | custom-call | tf_op jit(solution)/shard_map/layer/pallas_call | solution.py:713
  141.6 36.7 %merge.1 = bf16[32,16,416]{2,1,0:T(8,128)(2,1)} custom-call(bf16[4,832,128]{2,1,0:T(8,128)(2,1)} %get-tuple-element.7.lo, f32[1664]{0:T(1024)} %gain3.1, f32[1664]{0:T(1024)} %bias3.1, s32[4,256]{1,0:T(4,128)} %bitcast.11, s32[1,1024]{1,0:T(1,128)} %seg.3, s32[1,32]{1,0:T(1,128)} %owners.1, bf16[16,416,416]{2,1,0:T(8,128)(2,1)} %bitcast.7, f32[416]{0:T(512)} %pb.1), custom_call_target="tpu_custom_call" | custom-call | tf_op jit(solution)/shard_map/merge/pallas_call | solution.py:713
  178.3 1.9 %copy.22 = bf16[1,32,16,416]{3,2,1,0:T(8,128)(2,1)} copy(bf16[1,32,16,416]{3,2,1,0:T(8,128)(2,1)} %bitcast.8) | data formatting | bytes 851968
Async XLA Ops:
  0.0 1.6 collective-permute-start
  1.6 0.7 copy-start
